TPU v7x, 32 devices: a whole 2x2x4 slice. The times are simulated.
32 devices in a mesh: group: 8 (over y, x, core), shard: 4 (over z).
Axes of the slice: x: 2, y: 2, z: 4, core: 2. Of those that a mesh axis runs over, the one named last changes fastest.
Arguments:
- tokens: bfloat16 [2, 8, 2048, 768], P(None, 'group', 'shard'), may hold values from -6 to 6
- cond: float32 [2, 8, 128], P(None, 'group'), may hold values from -6 to 6
- seg_ids: int32 [2, 8, 2048], P(None, 'group'), may hold values from 0 to 12, as said below
- parents: int32 [2, 8, 13], P(None, 'group'), may hold values from 0 to 4, as said below
- cotangent: bfloat16 [2, 8, 2048, 768], P(None, 'group', 'shard'), may hold values from -6 to 6
- w_qkv: bfloat16 [768, 2304], P('shard'), may hold values from -0.21875 to 0.21875
- w_out: bfloat16 [768, 768], P('shard'), may hold values from -1.75 to 1.75
- w_fc1: bfloat16 [768, 3072], P('shard'), may hold values from -0.21875 to 0.21875
- b_fc1: bfloat16 [3072], P('shard'), may hold values from -3 to 3
- w_fc2: bfloat16 [3072, 768], P('shard'), may hold values from -0.109375 to 0.109375
- b_fc2: bfloat16 [768], P('shard'), may hold values from -3 to 3
- w_ada: bfloat16 [128, 4608], P(None, 'shard'), may hold values from -0.5 to 0.5
- b_ada: bfloat16 [4608], P('shard'), may hold values from -3 to 3
- gain1: bfloat16 [768], P('shard'), may hold values from 0.25 to 1.75
- gain2: bfloat16 [768], P('shard'), may hold values from 0.25 to 1.75
Outputs:
- out: bfloat16 [2, 8, 2048, 768], P(None, 'group', 'shard')
- grad_tokens: bfloat16 [2, 8, 2048, 768], P(None, 'group', 'shard')
- grad_cond: float32 [2, 8, 128], P(None, 'group')
- grad_w_qkv: float32 [768, 2304], P('shard')
- grad_w_out: float32 [768, 768], P('shard')
- grad_w_fc1: float32 [768, 3072], P('shard')
- grad_b_fc1: float32 [3072], P('shard')
- grad_w_fc2: float32 [3072, 768], P('shard')
- grad_b_fc2: float32 [768], P('shard')
- grad_w_ada: float32 [128, 4608], P(None, 'shard')
- grad_b_ada: float32 [4608], P('shard')
- grad_gain1: float32 [768], P('shard')
- grad_gain2: float32 [768], P('shard')
Inputs may be any that keep to these rules, and one draw needn't show every extreme that they name: `seg_ids`: along each tree's 2048 tokens the segment ids never fall, and every one of the 13 segments holds at least one token. In each tree segment 0 is the trunk with parents[0] = 0, segments 1 to 4 are branches with parent 0, and segments 5 to 12 are leaves, two on each branch.
All inputs are finite; a program needn't handle non-finite values.
Results may differ from a plain program's by a relative error of at most 0.02.
The roundings to bfloat16 on the way count: a program that leaves them out, or rounds other values in their place, can miss the bound.
Values may be sent and summed in bfloat16 or wider, within the bound.
No kernel may reach another device: no remote copies, remote signals or barrier semaphores. Data moves between devices by JAX's collectives and lax.ppermute only.
A program may use at most 256 MiB of HBM per device.

v0:
```python
import math

import jax
import jax.numpy as jnp
from jax import lax
from jax.sharding import PartitionSpec as P

HEADS = 12


EPS = 1e-05
GELU_C = 0.7978845608028654
GELU_K = 0.044715
HIGH = lax.Precision.HIGHEST
SPLIT_DIMS = (0, 0, 0, 0, 0, 0, 1, 0, 0, 0)


def path_mask(query_seg, key_seg, parent_row):
    segments = parent_row.shape[0]
    labels = jnp.arange(segments, dtype=jnp.int32)
    first_up = jnp.sum(
        jnp.where(query_seg[:, None] == labels[None, :], parent_row[None, :], 0), axis=1
    )
    second_up = jnp.sum(
        jnp.where(first_up[:, None] == labels[None, :], parent_row[None, :], 0), axis=1
    )
    key_segs = key_seg[None, :]
    return (
        (key_segs == query_seg[:, None])
        | (key_segs == first_up[:, None])
        | (key_segs == second_up[:, None])
    )


def layer_norm(values, gain):
    centred = values - jnp.mean(values, axis=-1, keepdims=True)
    inv_std = lax.rsqrt(jnp.mean(centred * centred, axis=-1, keepdims=True) + EPS)
    normed = centred * inv_std
    return (normed, inv_std, normed * gain)


def norm_back(grad_normed, normed, inv_std):
    first_mean = jnp.mean(grad_normed, axis=-1, keepdims=True)
    second = jnp.mean(grad_normed * normed, axis=-1, keepdims=True)
    return (grad_normed - first_mean - normed * second) * inv_std


def gelu_parts(pre_act):
    inner_arg = GELU_C * (pre_act + GELU_K * pre_act * pre_act * pre_act)
    tangent = jnp.tanh(inner_arg)
    gelu_value = 0.5 * pre_act * (1.0 + tangent)
    gelu_slope = 0.5 * (1.0 + tangent) + 0.5 * pre_act * (1.0 - tangent * tangent) * GELU_C * (
        1.0 + 3.0 * GELU_K * pre_act * pre_act
    )
    return (gelu_value, gelu_slope)


def col_dot(left_op, right_op):
    return lax.dot_general(
        left_op, right_op, (((0,), (0,)), ((), ())), preferred_element_type=jnp.float32
    )


def row_dot(left_op, right_op):
    return lax.dot_general(
        left_op, right_op, (((1,), (1,)), ((), ())), preferred_element_type=jnp.float32
    )


def on_device(
    tokens,
    cond,
    seg_ids,
    parents,
    cotangent,
    w_qkv,
    w_out,
    w_fc1,
    b_fc1,
    w_fc2,
    b_fc2,
    w_ada,
    b_ada,
    gain1,
    gain2,
):
    batches = tokens.shape[0]
    row_count = tokens.shape[2]
    model_width = tokens.shape[3]
    head_dim = model_width // HEADS
    score_scale = 1.0 / math.sqrt(head_dim)
    offset = lax.axis_index("shard") * row_count
    shards = lax.axis_size("shard")
    local_w = (w_qkv, w_out, w_fc1, b_fc1, w_fc2, b_fc2, w_ada, b_ada, gain1, gain2)
    full_shapes = []
    for weight, split_dim in zip(local_w, SPLIT_DIMS):
        shape_list = list(weight.shape)
        shape_list[split_dim] = shape_list[split_dim] * shards
        full_shapes.append(tuple(shape_list))
    start_acc = tuple((jnp.zeros(shape_row, jnp.float32) for shape_row in full_shapes))

    def one_batch(batch_idx, carry):
        outs, grads_x, cond_parts, accum = carry
        gathered = (
            lax.all_gather(w_qkv, "shard", axis=0, tiled=True),
            lax.all_gather(w_out, "shard", axis=0, tiled=True),
            lax.all_gather(w_fc1, "shard", axis=0, tiled=True),
            lax.all_gather(b_fc1, "shard", axis=0, tiled=True),
            lax.all_gather(w_fc2, "shard", axis=0, tiled=True),
            lax.all_gather(b_fc2, "shard", axis=0, tiled=True),
            lax.all_gather(w_ada, "shard", axis=1, tiled=True),
            lax.all_gather(b_ada, "shard", axis=0, tiled=True),
            lax.all_gather(gain1, "shard", axis=0, tiled=True),
            lax.all_gather(gain2, "shard", axis=0, tiled=True),
        )
        qkv_w, out_w, fc1_w, fc1_b, fc2_w, fc2_b, ada_w, ada_b, gain_one, gain_two = gathered
        tok_in = lax.dynamic_index_in_dim(tokens, batch_idx, 0, False)[0].astype(jnp.float32)
        grad_out = lax.dynamic_index_in_dim(cotangent, batch_idx, 0, False)[0].astype(jnp.float32)
        tree_seg = lax.dynamic_index_in_dim(seg_ids, batch_idx, 0, False)[0]
        parent_row = lax.dynamic_index_in_dim(parents, batch_idx, 0, False)[0]
        cond_row = lax.dynamic_index_in_dim(cond, batch_idx, 0, False)
        tree_len = tree_seg.shape[0]
        query_seg = lax.dynamic_slice_in_dim(tree_seg, offset, row_count)
        allowed = path_mask(query_seg, tree_seg, parent_row)
        ada_full = ada_w.astype(jnp.float32)
        ada = jnp.dot(cond_row, ada_full, precision=HIGH)[0] + ada_b.astype(jnp.float32)
        shift_one, scale_one, gate_one, shift_two, scale_two, gate_two = jnp.split(ada, 6)
        gain_a = gain_one.astype(jnp.float32)
        gain_b = gain_two.astype(jnp.float32)
        normed_one, inv_one, lifted_one = layer_norm(tok_in, gain_a)
        act_one = (lifted_one * (1.0 + scale_one) + shift_one).astype(jnp.bfloat16)
        qkv = jnp.dot(act_one, qkv_w, preferred_element_type=jnp.float32).astype(jnp.bfloat16)
        query_heads = qkv[:, :model_width].reshape(row_count, HEADS, head_dim).transpose(1, 0, 2)
        whole_kv = lax.all_gather(qkv[:, model_width:], "shard", axis=0, tiled=True)
        key_heads = whole_kv[:, :model_width].reshape(tree_len, HEADS, head_dim).transpose(1, 0, 2)
        val_heads = whole_kv[:, model_width:].reshape(tree_len, HEADS, head_dim).transpose(1, 0, 2)

        def head_forward(unused, items):
            q_h, k_h, v_h = items
            masked = jnp.where(allowed, row_dot(q_h, k_h) * score_scale, -1000000000.0)
            top_val = jnp.max(masked, axis=-1, keepdims=True)
            expo = jnp.exp(masked - top_val)
            row_total = jnp.sum(expo, axis=-1, keepdims=True)
            probs = expo / row_total
            head_out = jnp.dot(probs.astype(jnp.bfloat16), v_h, preferred_element_type=jnp.float32)
            return (unused, (head_out.astype(jnp.bfloat16), top_val + jnp.log(row_total)))

        unused_f, (attn_heads, log_totals) = lax.scan(
            head_forward, 0, (query_heads, key_heads, val_heads)
        )
        attn = attn_heads.transpose(1, 0, 2).reshape(row_count, model_width)
        branch_one = jnp.dot(attn, out_w, preferred_element_type=jnp.float32)
        middle = tok_in + gate_one * branch_one
        normed_two, inv_two, lifted_two = layer_norm(middle, gain_b)
        act_two = (lifted_two * (1.0 + scale_two) + shift_two).astype(jnp.bfloat16)
        pre_act = jnp.dot(act_two, fc1_w, preferred_element_type=jnp.float32) + fc1_b.astype(
            jnp.float32
        )
        gelu_value, gelu_slope = gelu_parts(pre_act)
        hidden = gelu_value.astype(jnp.bfloat16)
        branch_two = jnp.dot(hidden, fc2_w, preferred_element_type=jnp.float32) + fc2_b.astype(
            jnp.float32
        )
        result = (middle + gate_two * branch_two).astype(jnp.bfloat16)
        grad_y2 = (grad_out * gate_two).astype(jnp.bfloat16)
        d_gate_two = jnp.sum(grad_out * branch_two, axis=0)
        g_fc2 = col_dot(hidden, grad_y2)
        g_b2 = jnp.sum(grad_y2.astype(jnp.float32), axis=0)
        grad_pre = (row_dot(grad_y2, fc2_w) * gelu_slope).astype(jnp.bfloat16)
        g_fc1 = col_dot(act_two, grad_pre)
        g_b1 = jnp.sum(grad_pre.astype(jnp.float32), axis=0)
        grad_a2 = row_dot(grad_pre, fc1_w)
        d_shift_two = jnp.sum(grad_a2, axis=0)
        d_scale_two = jnp.sum(grad_a2 * lifted_two, axis=0)
        grad_h2 = grad_a2 * (1.0 + scale_two)
        g_gain2 = jnp.sum(grad_h2 * normed_two, axis=0)
        grad_mid = grad_out + norm_back(grad_h2 * gain_b, normed_two, inv_two)
        grad_y1 = (grad_mid * gate_one).astype(jnp.bfloat16)
        d_gate_one = jnp.sum(grad_mid * branch_one, axis=0)
        g_out = col_dot(attn, grad_y1)
        grad_attn = (
            row_dot(grad_y1, out_w)
            .astype(jnp.bfloat16)
            .reshape(row_count, HEADS, head_dim)
            .transpose(1, 0, 2)
        )

        def head_backward(unused, items):
            q_h, k_h, v_h, lse_h, da_h = items
            masked = jnp.where(allowed, row_dot(q_h, k_h) * score_scale, -1000000000.0)
            again = jnp.exp(masked - lse_h)
            grad_prob = row_dot(da_h, v_h)
            delta_row = jnp.sum(again * grad_prob, axis=-1, keepdims=True)
            grad_score = (again * (grad_prob - delta_row)).astype(jnp.bfloat16)
            grad_q = jnp.dot(grad_score, k_h, preferred_element_type=jnp.float32) * score_scale
            grad_k = col_dot(grad_score, q_h) * score_scale
            grad_v = col_dot(again.astype(jnp.bfloat16), da_h)
            return (unused, (grad_q, grad_k, grad_v))

        unused_b, (q_grads, k_grads, v_grads) = lax.scan(
            head_backward, 0, (query_heads, key_heads, val_heads, log_totals, grad_attn)
        )
        grad_q_rows = q_grads.transpose(1, 0, 2).reshape(row_count, model_width)
        tree_kv = jnp.concatenate(
            [
                k_grads.transpose(1, 0, 2).reshape(tree_len, model_width),
                v_grads.transpose(1, 0, 2).reshape(tree_len, model_width),
            ],
            axis=1,
        )
        local_kv = lax.psum_scatter(
            tree_kv.astype(jnp.bfloat16), "shard", scatter_dimension=0, tiled=True
        ).astype(jnp.float32)
        grad_qkv = jnp.concatenate([grad_q_rows, local_kv], axis=1).astype(jnp.bfloat16)
        g_qkv = col_dot(act_one, grad_qkv)
        grad_a1 = row_dot(grad_qkv, qkv_w)
        d_shift_one = jnp.sum(grad_a1, axis=0)
        d_scale_one = jnp.sum(grad_a1 * lifted_one, axis=0)
        grad_h1 = grad_a1 * (1.0 + scale_one)
        g_gain1 = jnp.sum(grad_h1 * normed_one, axis=0)
        grad_in = (grad_mid + norm_back(grad_h1 * gain_a, normed_one, inv_one)).astype(jnp.bfloat16)
        grad_ada = jnp.concatenate(
            [d_shift_one, d_scale_one, d_gate_one, d_shift_two, d_scale_two, d_gate_two]
        )
        cond_part = row_dot(grad_ada[None, :], ada_full)[0]
        g_ada = cond_row[0][:, None] * grad_ada[None, :]
        fresh = (g_qkv, g_out, g_fc1, g_b1, g_fc2, g_b2, g_ada, grad_ada, g_gain1, g_gain2)
        accum = tuple((total + term for total, term in zip(accum, fresh)))
        outs = lax.dynamic_update_index_in_dim(outs, result[None], batch_idx, 0)
        grads_x = lax.dynamic_update_index_in_dim(grads_x, grad_in[None], batch_idx, 0)
        cond_parts = lax.dynamic_update_index_in_dim(cond_parts, cond_part, batch_idx, 0)
        return (outs, grads_x, cond_parts, accum)

    start_carry = (
        jnp.zeros(tokens.shape, jnp.bfloat16),
        jnp.zeros(tokens.shape, jnp.bfloat16),
        jnp.zeros((batches, cond.shape[2]), jnp.float32),
        start_acc,
    )
    outs, grads_x, cond_parts, accum = lax.fori_loop(0, batches, one_batch, start_carry)
    a_qkv, a_out, a_fc1, a_b1, a_fc2, a_b2, a_ada, a_bada, a_gain1, a_gain2 = accum
    shares = (
        lax.psum_scatter(
            a_qkv.astype(jnp.bfloat16), "shard", scatter_dimension=0, tiled=True
        ).astype(jnp.float32),
        lax.psum_scatter(
            a_out.astype(jnp.bfloat16), "shard", scatter_dimension=0, tiled=True
        ).astype(jnp.float32),
        lax.psum_scatter(
            a_fc1.astype(jnp.bfloat16), "shard", scatter_dimension=0, tiled=True
        ).astype(jnp.float32),
        lax.psum_scatter(
            a_b1.astype(jnp.bfloat16), "shard", scatter_dimension=0, tiled=True
        ).astype(jnp.float32),
        lax.psum_scatter(
            a_fc2.astype(jnp.bfloat16), "shard", scatter_dimension=0, tiled=True
        ).astype(jnp.float32),
        lax.psum_scatter(
            a_b2.astype(jnp.bfloat16), "shard", scatter_dimension=0, tiled=True
        ).astype(jnp.float32),
        lax.psum_scatter(
            a_ada.astype(jnp.bfloat16), "shard", scatter_dimension=1, tiled=True
        ).astype(jnp.float32),
        lax.psum_scatter(
            a_bada.astype(jnp.bfloat16), "shard", scatter_dimension=0, tiled=True
        ).astype(jnp.float32),
        lax.psum_scatter(
            a_gain1.astype(jnp.bfloat16), "shard", scatter_dimension=0, tiled=True
        ).astype(jnp.float32),
        lax.psum_scatter(
            a_gain2.astype(jnp.bfloat16), "shard", scatter_dimension=0, tiled=True
        ).astype(jnp.float32),
    )
    h_qkv, h_out, h_fc1, h_b1, h_fc2, h_b2, h_ada, h_bada, h_gain1, h_gain2 = shares
    t_qkv, t_out, t_fc1, t_b1, t_fc2, t_b2, t_ada, t_bada, t_gain1, t_gain2 = lax.psum(
        (h_qkv, h_out, h_fc1, h_b1, h_fc2, h_b2, h_ada, h_bada, h_gain1, h_gain2), "group"
    )
    cond_total = lax.psum(cond_parts, "shard")
    return (
        outs,
        grads_x,
        cond_total[:, None, :],
        t_qkv,
        t_out,
        t_fc1,
        t_b1,
        t_fc2,
        t_b2,
        t_ada,
        t_bada,
        t_gain1,
        t_gain2,
    )


def solution(mesh):
    in_specs = (
        P(None, "group", "shard", None),
        P(None, "group", None),
        P(None, "group", None),
        P(None, "group", None),
        P(None, "group", "shard", None),
        P("shard", None),
        P("shard", None),
        P("shard", None),
        P("shard"),
        P("shard", None),
        P("shard"),
        P(None, "shard"),
        P("shard"),
        P("shard"),
        P("shard"),
    )
    out_specs = (
        P(None, "group", "shard", None),
        P(None, "group", "shard", None),
        P(None, "group", None),
        P("shard", None),
        P("shard", None),
        P("shard", None),
        P("shard"),
        P("shard", None),
        P("shard"),
        P(None, "shard"),
        P("shard"),
        P("shard"),
        P("shard"),
    )
    return jax.shard_map(
        on_device, mesh=mesh, in_specs=in_specs, out_specs=out_specs, check_vma=False
    )
```

profile of v0, /device:TPU:1, one launch (start us, length us, event | category | flops | bytes accessed | tf_op | source)
XLA Modules:
  0.0 1967.3 jit_solution(13355855105542980057)
XLA Ops:
  8.1 1488.8 %while.145 = (s32[]{:T(128)}, bf16[2,1,512,768]{3,2,1,0:T(8,128)(2,1)}, bf16[2,1,512,768]{3,2,1,0:T(8,128)(2,1)}, f32[2,128]{1,0:T(2,128)}, f32[768,2304]{1,0:T(...) while((s32[]{:T(128)}, ...), condition=%wide.region_29.30_spmd.clone, body=%wide.region_0.29_spmd.clone.sunk | while | flops 22868463616 | bytes 604327936 | solution.py:240
  10.6 11.3 all-gather.6
  26.4 10.4 all-reduce.15
  38.6 4.9 all-gather.15.cloned.1.call-done
  45.4 69.3 %all-gather.17.cloned.1.call-done = bf16[768,2304]{1,0:T(8,128)(2,1)} async-done(((bf16[192,2304]{1,0:T(8,128)(2,1)}), bf16[768,2304]{1,0:T(8,128)(2,1)}) %all-gather.17.cloned.1.call-update) | async-done | bytes 3538960 | tf_op jit(solution)/shard_map/while/body/eval_jaxpr/all_gather | solution.py:105
  114.6 4.2 convolution_convert_fusion.4
  123.8 10.6 all-gather.7
  136.3 99.7 %all-gather.19.cloned.1.call-done = bf16[2048,1536]{1,0:T(8,128)(2,1)} async-done(((bf16[512,1536]{1,0:T(8,128)(2,1)}), bf16[2048,1536]{1,0:T(8,128)(2,1)}) %all-gather.19.cloned.1.call-update) | async-done | bytes 6291472 | tf_op jit(solution)/shard_map/while/body/eval_jaxpr/all_gather | solution.py:134
  236.0 4.9 fusion.179
  241.0 4.8 copy.77
  245.7 6.6 copy.78
  255.3 6.6 copy.80
  262.0 69.6 %while.146 = (s32[]{:T(128)}, bf16[12,512,64]{1,2,0:T(8,128)(2,1)S(1)}, f32[12,512,1]{1,2,0:T(1,128)S(1)}, bf16[12,512,64]{2,1,0:T(8,128)(2,1)}, bf16[12,2048,64...) while((s32[]{:T(128)}, ...), condition=%wide.region_8.8_spmd.clone, body=%wide.region_5.7_spmd.clone.sunk | while | flops 282099200 | bytes 13865073 | solution.py:148
  332.5 3.6 fusion.181
  336.4 19.6 all-gather.25.cloned.1.call-done
  356.0 7.2 fusion.182
  363.2 82.1 %all-gather.23.cloned.1.call-done = bf16[3072,768]{1,0:T(8,128)(2,1)} async-done(((bf16[768,768]{1,0:T(8,128)(2,1)}), bf16[3072,768]{1,0:T(8,128)(2,1)}) %all-gather.23.cloned.1.call-update) | async-done | bytes 4718608 | tf_op jit(solution)/shard_map/while/body/eval_jaxpr/all_gather | solution.py:109
  445.3 9.4 convert_reduce_fusion.10
  460.5 4.0 fusion.183
  470.4 144.7 %while.147 = (s32[]{:T(128)}, bf16[12,512,64]{1,2,0:T(8,128)(2,1)}, bf16[12,2048,64]{1,2,0:T(8,128)(2,1)}, bf16[12,2048,64]{1,2,0:T(8,128)(2,1)}, bf16[12,512,64...) while((s32[]{:T(128)}, bf16[12,512,64]{1,2,0:T(8,128)(2,1)}, ...), condition=%wide.region_15.15_spmd.clone, body=%wide.region_13.14_spmd.clone.sunk | while | flops 685932032 | bytes 34632840 | solution.py:200
  615.1 6.7 pad_maximum_fusion.7
  622.6 3.5 select_add_fusion.19
  626.1 5.6 select_add_fusion.20
  631.8 6.8 select_add_fusion.22
  638.6 92.6 %reduce-scatter.19.cloned.1.call-done = bf16[512,1536]{0,1:T(8,128)(2,1)} async-done(((bf16[2048,1536]{0,1:T(8,128)(2,1)}), bf16[512,1536]{0,1:T(8,128)(2,1)}) %reduce-scatter.19.cloned.1.call-update) | async-done | bytes 1572880 | tf_op jit(solution)/shard_map/while/body/eval_jaxpr/reduce_scatter | solution.py:211
  731.3 6.6 fusion.184
  743.8 6.4 select_add_fusion.18
  752.7 10.8 all-gather.6
  768.0 9.2 all-reduce.15
  779.0 5.0 all-gather.15.cloned.1.call-done
  785.9 69.3 %all-gather.17.cloned.1.call-done = bf16[768,2304]{1,0:T(8,128)(2,1)} async-done(((bf16[192,2304]{1,0:T(8,128)(2,1)}), bf16[768,2304]{1,0:T(8,128)(2,1)}) %all-gather.17.cloned.1.call-update) | async-done | bytes 3538960 | tf_op jit(solution)/shard_map/while/body/eval_jaxpr/all_gather | solution.py:105
  855.1 4.2 convolution_convert_fusion.4
  864.7 10.8 all-gather.7
  877.3 99.2 %all-gather.19.cloned.1.call-done = bf16[2048,1536]{1,0:T(8,128)(2,1)} async-done(((bf16[512,1536]{1,0:T(8,128)(2,1)}), bf16[2048,1536]{1,0:T(8,128)(2,1)}) %all-gather.19.cloned.1.call-update) | async-done | bytes 6291472 | tf_op jit(solution)/shard_map/while/body/eval_jaxpr/all_gather | solution.py:134
  976.5 4.9 fusion.179
  981.5 4.7 copy.77
  986.2 6.6 copy.78
  995.8 6.6 copy.80
  1002.4 69.7 %while.146 = (s32[]{:T(128)}, bf16[12,512,64]{1,2,0:T(8,128)(2,1)S(1)}, f32[12,512,1]{1,2,0:T(1,128)S(1)}, bf16[12,512,64]{2,1,0:T(8,128)(2,1)}, bf16[12,2048,64...) while((s32[]{:T(128)}, ...), condition=%wide.region_8.8_spmd.clone, body=%wide.region_5.7_spmd.clone.sunk | while | flops 282099200 | bytes 13865073 | solution.py:148
  1073.0 3.6 fusion.181
  1076.9 19.8 %all-gather.25.cloned.1.call-done = bf16[768,3072]{1,0:T(8,128)(2,1)} async-done(((bf16[192,3072]{1,0:T(8,128)(2,1)}), bf16[768,3072]{1,0:T(8,128)(2,1)}) %all-gather.25.cloned.1.call-update) | async-done | bytes 4718608 | tf_op jit(solution)/shard_map/while/body/eval_jaxpr/all_gather | solution.py:107
  1096.7 7.2 fusion.182
  1103.9 82.3 %all-gather.23.cloned.1.call-done = bf16[3072,768]{1,0:T(8,128)(2,1)} async-done(((bf16[768,768]{1,0:T(8,128)(2,1)}), bf16[3072,768]{1,0:T(8,128)(2,1)}) %all-gather.23.cloned.1.call-update) | async-done | bytes 4718608 | tf_op jit(solution)/shard_map/while/body/eval_jaxpr/all_gather | solution.py:109
  1186.2 9.0 convert_reduce_fusion.10
  1195.2 3.2 multiply_reduce_fusion.10
  1201.0 4.0 fusion.183
  1210.8 144.8 %while.147 = (s32[]{:T(128)}, bf16[12,512,64]{1,2,0:T(8,128)(2,1)}, bf16[12,2048,64]{1,2,0:T(8,128)(2,1)}, bf16[12,2048,64]{1,2,0:T(8,128)(2,1)}, bf16[12,512,64...) while((s32[]{:T(128)}, bf16[12,512,64]{1,2,0:T(8,128)(2,1)}, ...), condition=%wide.region_15.15_spmd.clone, body=%wide.region_13.14_spmd.clone.sunk | while | flops 685932032 | bytes 34632840 | solution.py:200
  1355.6 6.7 pad_maximum_fusion.7
  1363.1 4.2 select_add_fusion.19
  1367.4 8.5 select_add_fusion.20
  1375.9 9.3 select_add_fusion.22
  1385.2 86.4 %reduce-scatter.19.cloned.1.call-done = bf16[512,1536]{0,1:T(8,128)(2,1)} async-done(((bf16[2048,1536]{0,1:T(8,128)(2,1)}), bf16[512,1536]{0,1:T(8,128)(2,1)}) %reduce-scatter.19.cloned.1.call-update) | async-done | bytes 1572880 | tf_op jit(solution)/shard_map/while/body/eval_jaxpr/reduce_scatter | solution.py:211
  1471.7 6.6 fusion.184
  1484.3 8.6 select_add_fusion.18
  1502.1 5.1 convert_element_type.317
  1507.3 6.6 convert_element_type.321
  1514.0 6.3 convert_element_type.325
  1523.7 9.8 psum.77
  1533.5 12.9 all-reduce.13
  1547.9 13.1 reduce-scatter.11.cloned.1.call-done
  1561.0 67.2 %reduce-scatter.9.cloned.1.call-done = bf16[192,2304]{1,0:T(8,128)(2,1)} async-done(((bf16[768,2304]{1,0:T(8,128)(2,1)}), bf16[192,2304]{1,0:T(8,128)(2,1)}) %reduce-scatter.9.cloned.1.call-update) | async-done | bytes 884752 | tf_op jit(solution)/shard_map/reduce_scatter | solution.py:243
  1628.2 88.0 %reduce-scatter.13.cloned.1.call-done = bf16[192,3072]{1,0:T(8,128)(2,1)} async-done(((bf16[768,3072]{1,0:T(8,128)(2,1)}), bf16[192,3072]{1,0:T(8,128)(2,1)}) %reduce-scatter.13.cloned.1.call-update) | async-done | bytes 1179664 | tf_op jit(solution)/shard_map/reduce_scatter | solution.py:249
  1716.3 88.0 %reduce-scatter.15.cloned.1.call-done = bf16[768,768]{1,0:T(8,128)(2,1)} async-done(((bf16[3072,768]{1,0:T(8,128)(2,1)}), bf16[768,768]{1,0:T(8,128)(2,1)}) %reduce-scatter.15.cloned.1.call-update) | async-done | bytes 1179664 | tf_op jit(solution)/shard_map/reduce_scatter | solution.py:255
  1804.3 155.3 %all-reduce.17 = (f32[192,2304]{1,0:T(8,128)}, f32[192,768]{1,0:T(8,128)}, f32[192,3072]{1,0:T(8,128)}, f32[768]{0:T(1024)}, f32[768,768]{1,0:T(8,128)}, /*index...) all-reduce(bf16[192,2304]{1,0:T(8,128)(2,1)} %reduce-scatter.9.clon, ...), channel_id=1, replica_groups=mesh['group'=8,'shard'=4] {'group'}, use_global_device_ids=true, to_apply=%region_32.33 | all-reduce | flops 1919424 | bytes 11521536 | tf_op jit(solution)/shard_map/psum | solution.py:275
  (705 shorter events, 509.4 us)
Async XLA Ops:
  8.4 29.8 %copy-start = (bf16[2,1,512,768]{3,2,1,0:T(8,128)(2,1)S(1)}, bf16[2,1,512,768]{3,2,1,0:T(8,128)(2,1)}, u32[]{:S(2)}) copy-start(bf16[2,1,512,768]{3,2,1,0:T(8,128)(2,1)} %get-tuple-element.1919) | copy-start | bytes 4718596 | tf_op jit(solution)/shard_map/while
  8.4 35.1 %copy-start.45 = (f32[2,1,128]{2,1,0:T(1,128)S(1)}, f32[2,1,128]{2,1,0:T(1,128)}, u32[]{:S(2)}) copy-start(f32[2,1,128]{2,1,0:T(1,128)} %get-tuple-element.1920) | copy-start | bytes 3076 | tf_op jit(solution)/shard_map/while
  8.4 35.1 %all-gather.15.cloned.1.call-start = ((), (), s32[]{:S(2)}) async-start(), calls=%async_computation.11 | async-start | bytes 1474560 | tf_op jit(solution)/shard_map/while/body/eval_jaxpr/all_gather | solution.py:111
  9.1 105.5 %all-gather.17.cloned.1.call-start = ((), (), s32[]{:S(2)}) async-start(), calls=%async_computation.12 | async-start | bytes 4423680 | tf_op jit(solution)/shard_map/while/body/eval_jaxpr/all_gather | solution.py:105
  9.9 226.1 %all-gather.19.cloned.1.call-start = ((), (), s32[]{:S(2)}) async-start(), calls=%async_computation.13 | async-start | bytes 7864320 | tf_op jit(solution)/shard_map/while/body/eval_jaxpr/all_gather | solution.py:134
  36.9 82.0 %copy-start.18 = (f32[768]{0:T(1024)}, f32[768]{0:T(1024)S(1)}, u32[]{:S(2)}) copy-start(f32[768]{0:T(1024)S(1)} %convert_element_type.523) | copy-start | bytes 9220 | tf_op jit(solution)/shard_map/while
  38.2 80.7 %copy-start.24 = (f32[512]{0:T(512)}, f32[512]{0:T(512)S(1)}, u32[]{:S(2)}) copy-start(f32[512]{0:T(512)S(1)} %broadcast_multiply_fusion.11) | copy-start | bytes 6148 | tf_op jit(solution)/shard_map/while
  38.6 80.3 %copy-start.26 = (f32[512]{0:T(512)}, f32[512]{0:T(512)S(1)}, u32[]{:S(2)}) copy-start(f32[512]{0:T(512)S(1)} %add_rsqrt_fusion.4) | copy-start | bytes 6148 | tf_op jit(solution)/shard_map/while
  45.4 73.5 %copy-start.20 = (f32[768]{0:T(1024)}, f32[768]{0:T(1024)S(1)}, u32[]{:S(2)}) copy-start(f32[768]{0:T(1024)S(1)} %get-tuple-element.1683) | copy-start | bytes 9220 | tf_op jit(solution)/shard_map/while
  45.4 73.5 %copy-start.22 = (f32[768]{0:T(1024)}, f32[768]{0:T(1024)S(1)}, u32[]{:S(2)}) copy-start(f32[768]{0:T(1024)S(1)} %get-tuple-element.1682) | copy-start | bytes 9220 | tf_op jit(solution)/shard_map/while
  121.6 12.8 slice-start
  121.6 210.0 %all-gather.21.cloned.1.call-start = ((), (), s32[]{:S(2)}) async-start(), calls=%async_computation.14 | async-start | bytes 1474560 | tf_op jit(solution)/shard_map/while/body/eval_jaxpr/all_gather | solution.py:106
  122.2 233.8 %all-gather.25.cloned.1.call-start = ((), (), s32[]{:S(2)}) async-start(), calls=%async_computation.16 | async-start | bytes 5898240 | tf_op jit(solution)/shard_map/while/body/eval_jaxpr/all_gather | solution.py:107
  122.8 322.5 %all-gather.23.cloned.1.call-start = ((), (), s32[]{:S(2)}) async-start(), calls=%async_computation.15 | async-start | bytes 5898240 | tf_op jit(solution)/shard_map/while/body/eval_jaxpr/all_gather | solution.py:109
  123.4 607.8 %reduce-scatter.19.cloned.1.call-start = ((), (), s32[]{:S(2)}) async-start(), calls=%async_computation.17 | async-start | bytes 7864320 | tf_op jit(solution)/shard_map/while/body/eval_jaxpr/reduce_scatter | solution.py:211
  255.3 6.6 copy-start.10
  262.0 70.6 %copy-start.1 = (bf16[2,1,512,768]{3,2,1,0:T(8,128)(2,1)S(1)}, bf16[2,1,512,768]{3,2,1,0:T(8,128)(2,1)}, u32[]{:S(2)}) copy-start(bf16[2,1,512,768]{3,2,1,0:T(8,128)(2,1)} %get-tuple-element.1919) | copy-start | bytes 4718596 | tf_op jit(solution)/shard_map/while
  356.0 89.3 %copy-start.15 = (bf16[2,1,512,768]{3,2,1,0:T(8,128)(2,1)S(1)}, bf16[2,1,512,768]{3,2,1,0:T(8,128)(2,1)}, u32[]{:S(2)}) copy-start(bf16[2,1,512,768]{3,2,1,0:T(8,128)(2,1)} %get-tuple-element.1934) | copy-start | bytes 4718596 | tf_op jit(solution)/shard_map/while
  445.3 9.4 copy-start.50
  454.8 5.8 copy-start.56
  622.6 9.1 slice-start.1
  631.7 99.5 %copy-start.2 = (bf16[2,1,512,768]{3,2,1,0:T(8,128)(2,1)S(1)}, bf16[2,1,512,768]{3,2,1,0:T(8,128)(2,1)}, u32[]{:S(2)}) copy-start(bf16[2,1,512,768]{3,2,1,0:T(8,128)(2,1)} %get-tuple-element.1919) | copy-start | bytes 4718596 | tf_op jit(solution)/shard_map/while
  631.7 99.5 %copy-start.19 = (f32[768]{0:T(1024)S(1)}, f32[768]{0:T(1024)}, u32[]{:S(2)}) copy-start(f32[768]{0:T(1024)} %copy-done.18) | copy-start | bytes 9220 | tf_op jit(solution)/shard_map/while
  631.7 99.5 %copy-start.21 = (f32[768]{0:T(1024)S(1)}, f32[768]{0:T(1024)}, u32[]{:S(2)}) copy-start(f32[768]{0:T(1024)} %copy-done.20) | copy-start | bytes 9220 | tf_op jit(solution)/shard_map/while
  631.7 99.5 %copy-start.25 = (f32[512]{0:T(512)S(1)}, f32[512]{0:T(512)}, u32[]{:S(2)}) copy-start(f32[512]{0:T(512)} %copy-done.24) | copy-start | bytes 6148 | tf_op jit(solution)/shard_map/while
  631.8 99.5 %copy-start.27 = (f32[512]{0:T(512)S(1)}, f32[512]{0:T(512)}, u32[]{:S(2)}) copy-start(f32[512]{0:T(512)} %copy-done.26) | copy-start | bytes 6148 | tf_op jit(solution)/shard_map/while
  731.2 6.7 copy-start.41
  731.2 6.8 copy-start.28
  731.3 6.8 copy-start.6
  750.5 28.1 %copy-start = (bf16[2,1,512,768]{3,2,1,0:T(8,128)(2,1)S(1)}, bf16[2,1,512,768]{3,2,1,0:T(8,128)(2,1)}, u32[]{:S(2)}) copy-start(bf16[2,1,512,768]{3,2,1,0:T(8,128)(2,1)} %get-tuple-element.1919) | copy-start | bytes 4718596 | tf_op jit(solution)/shard_map/while
  750.5 33.5 %copy-start.45 = (f32[2,1,128]{2,1,0:T(1,128)S(1)}, f32[2,1,128]{2,1,0:T(1,128)}, u32[]{:S(2)}) copy-start(f32[2,1,128]{2,1,0:T(1,128)} %get-tuple-element.1920) | copy-start | bytes 3076 | tf_op jit(solution)/shard_map/while
  750.5 33.5 %all-gather.15.cloned.1.call-start = ((), (), s32[]{:S(2)}) async-start(), calls=%async_computation.11 | async-start | bytes 1474560 | tf_op jit(solution)/shard_map/while/body/eval_jaxpr/all_gather | solution.py:111
  751.2 103.9 %all-gather.17.cloned.1.call-start = ((), (), s32[]{:S(2)}) async-start(), calls=%async_computation.12 | async-start | bytes 4423680 | tf_op jit(solution)/shard_map/while/body/eval_jaxpr/all_gather | solution.py:105
  752.0 224.5 %all-gather.19.cloned.1.call-start = ((), (), s32[]{:S(2)}) async-start(), calls=%async_computation.13 | async-start | bytes 7864320 | tf_op jit(solution)/shard_map/while/body/eval_jaxpr/all_gather | solution.py:134
  777.3 82.1 %copy-start.18 = (f32[768]{0:T(1024)}, f32[768]{0:T(1024)S(1)}, u32[]{:S(2)}) copy-start(f32[768]{0:T(1024)S(1)} %convert_element_type.523) | copy-start | bytes 9220 | tf_op jit(solution)/shard_map/while
  778.6 80.8 %copy-start.24 = (f32[512]{0:T(512)}, f32[512]{0:T(512)S(1)}, u32[]{:S(2)}) copy-start(f32[512]{0:T(512)S(1)} %broadcast_multiply_fusion.11) | copy-start | bytes 6148 | tf_op jit(solution)/shard_map/while
  779.0 80.4 %copy-start.26 = (f32[512]{0:T(512)}, f32[512]{0:T(512)S(1)}, u32[]{:S(2)}) copy-start(f32[512]{0:T(512)S(1)} %add_rsqrt_fusion.4) | copy-start | bytes 6148 | tf_op jit(solution)/shard_map/while
  785.9 73.5 %copy-start.20 = (f32[768]{0:T(1024)}, f32[768]{0:T(1024)S(1)}, u32[]{:S(2)}) copy-start(f32[768]{0:T(1024)S(1)} %get-tuple-element.1683) | copy-start | bytes 9220 | tf_op jit(solution)/shard_map/while
  785.9 73.5 %copy-start.22 = (f32[768]{0:T(1024)}, f32[768]{0:T(1024)S(1)}, u32[]{:S(2)}) copy-start(f32[768]{0:T(1024)S(1)} %get-tuple-element.1682) | copy-start | bytes 9220 | tf_op jit(solution)/shard_map/while
  862.1 13.4 slice-start
  862.2 210.0 %all-gather.21.cloned.1.call-start = ((), (), s32[]{:S(2)}) async-start(), calls=%async_computation.14 | async-start | bytes 1474560 | tf_op jit(solution)/shard_map/while/body/eval_jaxpr/all_gather | solution.py:106
  862.9 233.8 %all-gather.25.cloned.1.call-start = ((), (), s32[]{:S(2)}) async-start(), calls=%async_computation.16 | async-start | bytes 5898240 | tf_op jit(solution)/shard_map/while/body/eval_jaxpr/all_gather | solution.py:107
  863.5 322.7 %all-gather.23.cloned.1.call-start = ((), (), s32[]{:S(2)}) async-start(), calls=%async_computation.15 | async-start | bytes 5898240 | tf_op jit(solution)/shard_map/while/body/eval_jaxpr/all_gather | solution.py:109
  864.2 607.4 %reduce-scatter.19.cloned.1.call-start = ((), (), s32[]{:S(2)}) async-start(), calls=%async_computation.17 | async-start | bytes 7864320 | tf_op jit(solution)/shard_map/while/body/eval_jaxpr/reduce_scatter | solution.py:211
  995.8 6.6 copy-start.10
  1002.4 70.6 %copy-start.1 = (bf16[2,1,512,768]{3,2,1,0:T(8,128)(2,1)S(1)}, bf16[2,1,512,768]{3,2,1,0:T(8,128)(2,1)}, u32[]{:S(2)}) copy-start(bf16[2,1,512,768]{3,2,1,0:T(8,128)(2,1)} %get-tuple-element.1919) | copy-start | bytes 4718596 | tf_op jit(solution)/shard_map/while
  1096.7 89.5 %copy-start.15 = (bf16[2,1,512,768]{3,2,1,0:T(8,128)(2,1)S(1)}, bf16[2,1,512,768]{3,2,1,0:T(8,128)(2,1)}, u32[]{:S(2)}) copy-start(bf16[2,1,512,768]{3,2,1,0:T(8,128)(2,1)} %get-tuple-element.1934) | copy-start | bytes 4718596 | tf_op jit(solution)/shard_map/while
  1186.2 9.0 copy-start.50
  1363.1 12.8 slice-start.1
  1367.3 8.6 copy-start.17
  1367.3 8.5 slice-start.2
  1375.9 95.8 %copy-start.2 = (bf16[2,1,512,768]{3,2,1,0:T(8,128)(2,1)S(1)}, bf16[2,1,512,768]{3,2,1,0:T(8,128)(2,1)}, u32[]{:S(2)}) copy-start(bf16[2,1,512,768]{3,2,1,0:T(8,128)(2,1)} %get-tuple-element.1919) | copy-start | bytes 4718596 | tf_op jit(solution)/shard_map/while
  1375.9 95.7 %copy-start.19 = (f32[768]{0:T(1024)S(1)}, f32[768]{0:T(1024)}, u32[]{:S(2)}) copy-start(f32[768]{0:T(1024)} %copy-done.18) | copy-start | bytes 9220 | tf_op jit(solution)/shard_map/while
  1375.9 95.7 %copy-start.21 = (f32[768]{0:T(1024)S(1)}, f32[768]{0:T(1024)}, u32[]{:S(2)}) copy-start(f32[768]{0:T(1024)} %copy-done.20) | copy-start | bytes 9220 | tf_op jit(solution)/shard_map/while
  1375.9 95.7 %copy-start.25 = (f32[512]{0:T(512)S(1)}, f32[512]{0:T(512)}, u32[]{:S(2)}) copy-start(f32[512]{0:T(512)} %copy-done.24) | copy-start | bytes 6148 | tf_op jit(solution)/shard_map/while
  1375.9 95.7 %copy-start.27 = (f32[512]{0:T(512)S(1)}, f32[512]{0:T(512)}, u32[]{:S(2)}) copy-start(f32[512]{0:T(512)} %copy-done.26) | copy-start | bytes 6148 | tf_op jit(solution)/shard_map/while
  1471.7 6.7 copy-start.41
  1471.7 6.8 copy-start.28
  1471.7 6.8 copy-start.6
  1497.0 49.8 %reduce-scatter.17.cloned.1.call-start = ((), (), s32[]{:S(2)}) async-start(), calls=%async_computation.10 | async-start | bytes 1474560
  1500.3 60.8 %reduce-scatter.11.cloned.1.call-start = ((), (), s32[]{:S(2)}) async-start(), calls=%async_computation.7 | async-start | bytes 1474560 | tf_op jit(solution)/shard_map/reduce_scatter | solution.py:246
  1502.1 126.2 %reduce-scatter.9.cloned.1.call-start = ((), (), s32[]{:S(2)}) async-start(), calls=%async_computation.6 | async-start | bytes 4423680 | tf_op jit(solution)/shard_map/reduce_scatter | solution.py:243
  1507.3 209.0 %reduce-scatter.13.cloned.1.call-start = ((), (), s32[]{:S(2)}) async-start(), calls=%async_computation.8 | async-start | bytes 5898240 | tf_op jit(solution)/shard_map/reduce_scatter | solution.py:249
  1514.0 290.3 %reduce-scatter.15.cloned.1.call-start = ((), (), s32[]{:S(2)}) async-start(), calls=%async_computation.9 | async-start | bytes 5898240 | tf_op jit(solution)/shard_map/reduce_scatter | solution.py:255
  (67 other events, 156.7 us)
Sparse Core Ops, SparseCore 0:
  10.8 32.5 all-gather.14
  45.1 69.5 all-gather.16
  121.8 114.2 all-gather.18
  237.5 27.8 all-gather.20
  266.8 89.1 all-gather.24
  357.4 87.8 all-gather.22
  622.0 109.1 reduce-scatter.18
  752.9 31.0 all-gather.14
  785.6 69.5 all-gather.16
  862.3 114.1 all-gather.18
  978.1 27.9 all-gather.20
  1007.5 89.1 all-gather.24
  1098.2 87.8 all-gather.22
  1362.4 109.1 reduce-scatter.18
Sparse Core Ops, SparseCore 1:
  1500.3 29.3 reduce-scatter.16
  1532.4 28.5 reduce-scatter.10
  1563.2 65.0 reduce-scatter.8
  1630.6 85.6 reduce-scatter.12
  1718.6 85.6 reduce-scatter.14
where the time goes:
time: 1980 us; the launch traced here: 1970 us
  waiting for transfers between devices  993 us (50%)
  matrix products  536 us (27%)
  blocking collectives  241 us (12%)
  local copies, waits for them, and re-layouts  92.8 us (5%)
  other arithmetic  76.5 us (4%)
    dot_general x82, matrix products, row_dot(): lax.dot_general(left_op, right_op, (((1,), (1,)), ((), ())), preferred_el...  231 us
    all_gather x2, waiting for transfers between devices, one_batch(): whole_kv = lax.all_gather(qkv[:, model_width:], 'shard', axis=0, tiled=True)  199 us
    reduce_scatter x2, waiting for transfers between devices, one_batch(): lax.psum_scatter(tree_kv.astype(jnp.bfloat16), 'shard', scatter_dimension...  179 us
    all_gather x2, waiting for transfers between devices, one_batch(): lax.all_gather(w_fc2, 'shard', axis=0, tiled=True)  164 us
    psum x1, blocking collectives, on_device(): lax.psum((h_qkv, h_out, h_fc1, h_b1, h_fc2, h_b2, h_ada, h_bada, h_gain1,...  155 us
    dot_general x56, matrix products, col_dot(): lax.dot_general(left_op, right_op, (((0,), (0,)), ((), ())), preferred_el...  153 us
    all_gather x2, waiting for transfers between devices, one_batch(): lax.all_gather(w_qkv, 'shard', axis=0, tiled=True)  139 us
    reduce_scatter x1, waiting for transfers between devices, on_device(): lax.psum_scatter(a_fc2.astype(jnp.bfloat16), 'shard', scatter_dimension=0...  88 us
  transfers between devices with their start and end apart: 19, of which 16 were waited for; matrix products, arithmetic and copies ran while one was open for 15% of the time, Pallas kernels for 0%

commit v1 on v0

v1 whole, which is shorter than its diff:
```python
import math

import jax
import jax.numpy as jnp
from jax import lax
from jax.sharding import PartitionSpec as P

HEADS = 12
EPS = 1e-05
GELU_C = 0.7978845608028654
GELU_K = 0.044715
HIGH = lax.Precision.HIGHEST
BF = jnp.bfloat16
F32 = jnp.float32


def layer_norm(values):
    centred = values - jnp.mean(values, axis=-1, keepdims=True)
    inv_std = lax.rsqrt(jnp.mean(centred * centred, axis=-1, keepdims=True) + EPS)
    return centred * inv_std, inv_std


def norm_back(grad_normed, normed, inv_std):
    first_mean = jnp.mean(grad_normed, axis=-1, keepdims=True)
    second = jnp.mean(grad_normed * normed, axis=-1, keepdims=True)
    return (grad_normed - first_mean - normed * second) * inv_std


def gelu_parts(pre_act):
    inner_arg = GELU_C * (pre_act + GELU_K * pre_act * pre_act * pre_act)
    tangent = jnp.tanh(inner_arg)
    gelu_value = 0.5 * pre_act * (1.0 + tangent)
    gelu_slope = 0.5 * (1.0 + tangent) + 0.5 * pre_act * (1.0 - tangent * tangent) * GELU_C * (
        1.0 + 3.0 * GELU_K * pre_act * pre_act
    )
    return gelu_value, gelu_slope


def mm(left, right):
    return jnp.dot(left, right, preferred_element_type=F32)


def mm_t(left, right):
    return lax.dot_general(left, right, (((1,), (1,)), ((), ())), preferred_element_type=F32)


def t_mm(left, right):
    return lax.dot_general(left, right, (((0,), (0,)), ((), ())), preferred_element_type=F32)


class Links:
    def __init__(self, groups, shards):
        self.groups, self.shards, self.planes = groups, shards, groups // 2
        self.g = lax.axis_index("group")
        self.s = lax.axis_index("shard")
        self.c = self.g % 2
        self.plane = self.g // 2

    def swap(self, value):
        return lax.ppermute(value, "group", [(i, i ^ 1) for i in range(self.groups)])

    def turn(self, value, step):
        n = self.shards
        return lax.ppermute(value, "shard", [(i, (i + step) % n) for i in range(n)])

    def across(self, value, step):
        return lax.ppermute(value, "group", [(i, i ^ (2 * step)) for i in range(self.groups)])

    def round_perm(self, k):
        n, perm = self.shards, []
        for g in range(self.groups):
            for s in range(n):
                d = (s + k) % n
                goal = ((g // 2) * 2 + d % 2, 2 * (d // 2) + g % 2)
                perm.append((g * n + s, goal[0] * n + goal[1]))
        return perm

    def to_trees(self, value):
        batches, rows, width = value.shape
        pieces = value.reshape(batches * 2, rows // 2, width)
        got = []
        for k in range(self.shards):
            piece = lax.dynamic_index_in_dim(pieces, (self.s + k) % self.shards, 0, False)
            got.append(lax.ppermute(piece, ("group", "shard"), self.round_perm(k)))
        return jnp.concatenate(got, axis=0)

    def from_trees(self, value, batches):
        total, width = value.shape
        rows = total // self.shards
        out = jnp.zeros((self.shards, rows, width), value.dtype)
        for k in range(self.shards):
            back = [(b, a) for a, b in self.round_perm(k)]
            piece = lax.ppermute(value[k * rows : (k + 1) * rows], ("group", "shard"), back)
            out = lax.dynamic_update_index_in_dim(out, piece, (self.s + k) % self.shards, 0)
        return out.reshape(batches, 1, 2 * rows, width)

    def line_order(self, parts):
        stacked = jnp.stack(parts)
        return jnp.stack(
            [
                lax.dynamic_index_in_dim(stacked, (self.s - j) % self.shards, 0, False)
                for j in range(self.shards)
            ]
        )

    def line_gather(self, value):
        return self.line_order([value] + [self.turn(value, k) for k in range(1, self.shards)])

    def gather_weight(self, weight):
        rows = weight.shape[0] // self.groups
        part = lax.dynamic_slice_in_dim(weight, self.g * rows, rows, 0)
        return lax.all_gather(part, ("shard", "group"), axis=0, tiled=True)

    def plane_sum(self, value):
        if self.planes != 4:
            groups = [[2 * p + c for p in range(self.planes)] for c in range(2)]
            return lax.psum_scatter(
                value, "group", scatter_dimension=1, axis_index_groups=groups
            ).astype(F32)
        total = lax.dynamic_index_in_dim(value, self.plane, 1, False).astype(F32)
        for k in range(1, 4):
            piece = lax.dynamic_index_in_dim(value, self.plane ^ k, 1, False)
            total = total + self.across(piece, k).astype(F32)
        return total

    def plane_gather(self, value):
        if self.planes != 4:
            groups = [[2 * p + c for p in range(self.planes)] for c in range(2)]
            return lax.all_gather(value, "group", axis_index_groups=groups)
        parts = jnp.stack([value] + [self.across(value, k) for k in range(1, 4)])
        return jnp.stack(
            [lax.dynamic_index_in_dim(parts, self.plane ^ j, 0, False) for j in range(4)]
        )

    def reduce_grad(self, grad):
        width = grad.shape[1]
        rows = grad.shape[0] // self.shards
        halves = grad.reshape(self.shards, 2, rows // 2, width)
        mine = lax.dynamic_index_in_dim(halves, self.c, 1, False)
        yours = lax.dynamic_index_in_dim(halves, 1 - self.c, 1, False)
        pair = (mine.astype(F32) + self.swap(yours).astype(F32)).astype(BF)
        fine = rows // 2 // self.planes
        plane = self.plane_sum(pair.reshape(self.shards, self.planes, fine, width)).astype(BF)
        total = lax.dynamic_index_in_dim(plane, self.s, 0, False).astype(F32)
        for k in range(1, self.shards):
            piece = lax.dynamic_index_in_dim(plane, (self.s + k) % self.shards, 0, False)
            total = total + self.turn(piece, k).astype(F32)
        half = self.plane_gather(total.astype(BF)).reshape(rows // 2, width)
        other = self.swap(half)
        out = jnp.where(
            self.c == 0, jnp.concatenate([half, other]), jnp.concatenate([other, half])
        )
        return out.astype(F32)

    def tree_sums(self, vec):
        line = self.line_gather(vec)
        return line + self.swap(line)


def on_device(
    tokens,
    cond,
    seg_ids,
    parents,
    cotangent,
    w_qkv,
    w_out,
    w_fc1,
    b_fc1,
    w_fc2,
    b_fc2,
    w_ada,
    b_ada,
    gain1,
    gain2,
    groups,
):
    batches, _, row_count, width = tokens.shape
    shards = lax.axis_size("shard")
    assert shards == 2 * batches and groups % 2 == 0
    head_dim = width // HEADS
    scale = 1.0 / math.sqrt(head_dim)
    net = Links(groups, shards)
    rows = row_count // 2
    mine = shards * rows
    tree_len = seg_ids.shape[2]
    labels = parents.shape[2]
    cond_dim = cond.shape[2]

    qkv_w = net.gather_weight(w_qkv)
    tok = net.to_trees(tokens[:, 0])
    out_w = net.gather_weight(w_out)
    fc1_w = net.gather_weight(w_fc1)
    fc2_w = net.gather_weight(w_fc2)
    grad_out = net.to_trees(cotangent[:, 0])

    packed = jnp.concatenate(
        [seg_ids[:, 0].astype(F32), parents[:, 0].astype(F32), cond[:, 0]], axis=1
    )
    other = net.swap(packed)
    trees = jnp.where(
        net.c == 0, jnp.stack([packed, other], axis=1), jnp.stack([other, packed], axis=1)
    ).reshape(shards, packed.shape[1])
    conds = trees[:, tree_len + labels :]
    my_tree = lax.dynamic_index_in_dim(trees, net.s, 0, False)
    tree_seg = my_tree[:tree_len]
    parent_row = my_tree[tree_len : tree_len + labels]
    ada_rows = jnp.dot(conds, w_ada.astype(F32), precision=HIGH) + b_ada.astype(F32)
    small = jnp.concatenate([b_fc1, b_fc2, gain1, gain2]).astype(F32)
    pieces = jnp.concatenate(
        [ada_rows, jnp.broadcast_to(small[None], (shards, small.shape[0]))], axis=1
    )
    got = [lax.dynamic_index_in_dim(pieces, net.s, 0, False)]
    for k in range(1, shards):
        piece = lax.dynamic_index_in_dim(pieces, (net.s + k) % shards, 0, False)
        got.append(net.turn(piece, k))
    line = net.line_order(got)
    cut = ada_rows.shape[1]
    ada = line[:, :cut].reshape(-1)
    ends = [cut]
    for vec in (b_fc1, b_fc2, gain1, gain2):
        ends.append(ends[-1] + vec.shape[0])
    fc1_b, fc2_b, gain_a, gain_b = (
        line[:, ends[i] : ends[i + 1]].reshape(-1) for i in range(4)
    )
    shift_one, scale_one, gate_one, shift_two, scale_two, gate_two = jnp.split(ada, 6)

    half_seg = tree_seg.reshape(shards, 2, rows)
    base = 2 * (net.s // 2)

    def row_segs(place):
        take = lax.dynamic_index_in_dim(half_seg, place, 1, False)
        return jnp.concatenate(
            [
                lax.dynamic_index_in_dim(take, (base + place - k) % shards, 0, False)
                for k in range(shards)
            ]
        )

    query_seg = row_segs(net.c)
    key_seg = jnp.concatenate([query_seg, row_segs(1 - net.c)])
    label_row = jnp.arange(labels, dtype=F32)

    def parent_of(seg):
        return jnp.sum(
            jnp.where(seg[:, None] == label_row[None, :], parent_row[None, :], 0.0), axis=1
        )

    first_up = parent_of(query_seg)
    second_up = parent_of(first_up)
    allowed = (
        (key_seg[None, :] == query_seg[:, None])
        | (key_seg[None, :] == first_up[:, None])
        | (key_seg[None, :] == second_up[:, None])
    )

    tok_f = tok.astype(F32)
    normed_one, inv_one = layer_norm(tok_f)
    lifted_one = normed_one * gain_a
    act_one = (lifted_one * (1.0 + scale_one) + shift_one).astype(BF)
    qkv = mm(act_one, qkv_w).astype(BF)
    kv = qkv[:, width:]
    whole_kv = jnp.concatenate([kv, net.swap(kv)], axis=0)

    def heads_of(x):
        return x.reshape(x.shape[0], HEADS, head_dim).transpose(1, 0, 2)

    query_heads = heads_of(qkv[:, :width])
    key_heads = heads_of(whole_kv[:, :width])
    val_heads = heads_of(whole_kv[:, width:])

    def head_forward(unused, items):
        q_h, k_h, v_h = items
        masked = jnp.where(allowed, mm_t(q_h, k_h) * scale, -1000000000.0)
        top_val = jnp.max(masked, axis=-1, keepdims=True)
        expo = jnp.exp(masked - top_val)
        row_total = jnp.sum(expo, axis=-1, keepdims=True)
        probs = expo / row_total
        head_out = mm(probs.astype(BF), v_h)
        return unused, (head_out.astype(BF), top_val + jnp.log(row_total))

    _, (attn_heads, log_totals) = lax.scan(head_forward, 0, (query_heads, key_heads, val_heads))
    attn = attn_heads.transpose(1, 0, 2).reshape(mine, width)
    branch_one = mm(attn, out_w)
    middle = tok_f + gate_one * branch_one
    normed_two, inv_two = layer_norm(middle)
    lifted_two = normed_two * gain_b
    act_two = (lifted_two * (1.0 + scale_two) + shift_two).astype(BF)
    pre_act = mm(act_two, fc1_w) + fc1_b
    gelu_value, gelu_slope = gelu_parts(pre_act)
    hidden = gelu_value.astype(BF)
    branch_two = mm(hidden, fc2_w) + fc2_b
    out = net.from_trees((middle + gate_two * branch_two).astype(BF), batches)

    grad_f = grad_out.astype(F32)
    grad_y2 = (grad_f * gate_two).astype(BF)
    d_gate_two = jnp.sum(grad_f * branch_two, axis=0)
    t_fc2 = net.reduce_grad(t_mm(hidden, grad_y2).astype(BF))
    g_b2 = jnp.sum(grad_y2.astype(F32), axis=0)
    grad_pre = (mm_t(grad_y2, fc2_w) * gelu_slope).astype(BF)
    t_fc1 = net.reduce_grad(t_mm(act_two, grad_pre).astype(BF))
    g_b1 = jnp.sum(grad_pre.astype(F32), axis=0)
    grad_a2 = mm_t(grad_pre, fc1_w)
    d_shift_two = jnp.sum(grad_a2, axis=0)
    d_scale_two = jnp.sum(grad_a2 * lifted_two, axis=0)
    grad_h2 = grad_a2 * (1.0 + scale_two)
    g_gain2 = jnp.sum(grad_h2 * normed_two, axis=0)
    grad_mid = grad_f + norm_back(grad_h2 * gain_b, normed_two, inv_two)
    grad_y1 = (grad_mid * gate_one).astype(BF)
    d_gate_one = jnp.sum(grad_mid * branch_one, axis=0)
    t_out = net.reduce_grad(t_mm(attn, grad_y1).astype(BF))
    grad_attn = heads_of(mm_t(grad_y1, out_w).astype(BF))

    def head_backward(unused, items):
        q_h, k_h, v_h, lse_h, da_h = items
        masked = jnp.where(allowed, mm_t(q_h, k_h) * scale, -1000000000.0)
        again = jnp.exp(masked - lse_h)
        grad_prob = mm_t(da_h, v_h)
        delta_row = jnp.sum(again * grad_prob, axis=-1, keepdims=True)
        grad_score = (again * (grad_prob - delta_row)).astype(BF)
        grad_q = mm(grad_score, k_h) * scale
        grad_k = t_mm(grad_score, q_h) * scale
        grad_v = t_mm(again.astype(BF), da_h)
        return unused, (grad_q.astype(BF), grad_k, grad_v)

    _, (q_grads, k_grads, v_grads) = lax.scan(
        head_backward, 0, (query_heads, key_heads, val_heads, log_totals, grad_attn)
    )

    def rows_of(x):
        return x.transpose(1, 0, 2).reshape(x.shape[1], width)

    tree_kv = jnp.concatenate([rows_of(k_grads), rows_of(v_grads)], axis=1)
    local_kv = tree_kv[:mine] + net.swap(tree_kv[mine:].astype(BF)).astype(F32)
    grad_qkv = jnp.concatenate([rows_of(q_grads), local_kv.astype(BF)], axis=1)
    t_qkv = net.reduce_grad(t_mm(act_one, grad_qkv).astype(BF))
    grad_a1 = mm_t(grad_qkv, qkv_w)
    d_shift_one = jnp.sum(grad_a1, axis=0)
    d_scale_one = jnp.sum(grad_a1 * lifted_one, axis=0)
    grad_h1 = grad_a1 * (1.0 + scale_one)
    g_gain1 = jnp.sum(grad_h1 * normed_one, axis=0)
    grad_in = grad_mid + norm_back(grad_h1 * gain_a, normed_one, inv_one)
    grads_x = net.from_trees(grad_in.astype(BF), batches)

    early = net.tree_sums(
        jnp.concatenate([d_gate_one, d_shift_two, d_scale_two, d_gate_two, g_gain2, g_b2, g_b1])
    )
    late = net.tree_sums(jnp.concatenate([d_shift_one, d_scale_one, g_gain1]))
    dada = jnp.concatenate([late[:, : 2 * width], early[:, : 4 * width]], axis=1)
    bias = jnp.concatenate([early[:, 4 * width :], late[:, 2 * width :]], axis=1)
    everyone = net.plane_gather(
        jnp.concatenate([dada, conds, jnp.broadcast_to(jnp.sum(bias, axis=0), bias.shape)], axis=1)
    )
    every_dada = everyone[:, :, : 6 * width].reshape(-1, 6 * width)
    every_cond = everyone[:, :, 6 * width : 6 * width + cond_dim].reshape(-1, cond_dim)
    sums = jnp.sum(everyone[:, 0, 6 * width + cond_dim :], axis=0)

    def place(vec):
        n = vec.shape[-1] // shards
        return lax.dynamic_slice_in_dim(vec, net.s * n, n, vec.ndim - 1)

    dada_here = place(every_dada)
    t_ada = lax.dot_general(
        every_cond, dada_here, (((0,), (0,)), ((), ())), precision=HIGH
    )
    t_bada = jnp.sum(dada_here, axis=0)
    g_two, g_bias2, g_bias1, g_one = jnp.split(
        sums, [width, 2 * width, 2 * width + 4 * width]
    )
    own = lax.dynamic_index_in_dim(
        place(dada).reshape(batches, 2, -1), net.c, 1, False
    )
    cond_part = lax.dot_general(
        own, w_ada.astype(F32), (((1,), (1,)), ((), ())), precision=HIGH
    )
    cond_total = cond_part
    for k in range(1, shards):
        cond_total = cond_total + net.turn(cond_part, k)
    return (
        out,
        grads_x,
        cond_total[:, None, :],
        t_qkv,
        t_out,
        t_fc1,
        place(g_bias1),
        t_fc2,
        place(g_bias2),
        t_ada,
        t_bada,
        place(g_one),
        place(g_two),
    )


def solution(mesh):
    in_specs = (
        P(None, "group", "shard", None),
        P(None, "group", None),
        P(None, "group", None),
        P(None, "group", None),
        P(None, "group", "shard", None),
        P("shard", None),
        P("shard", None),
        P("shard", None),
        P("shard"),
        P("shard", None),
        P("shard"),
        P(None, "shard"),
        P("shard"),
        P("shard"),
        P("shard"),
    )
    out_specs = (
        P(None, "group", "shard", None),
        P(None, "group", "shard", None),
        P(None, "group", None),
        P("shard", None),
        P("shard", None),
        P("shard", None),
        P("shard"),
        P("shard", None),
        P("shard"),
        P(None, "shard"),
        P("shard"),
        P("shard"),
        P("shard"),
    )
    groups = mesh.shape["group"]

    def run(*args):
        return on_device(*args, groups)

    return jax.shard_map(
        run, mesh=mesh, in_specs=in_specs, out_specs=out_specs, check_vma=False
    )
```

time: 1980 us -> 1020 us (0.52)
  waiting for transfers between devices: 993 us -> 133 us
  blocking collectives: 241 us -> 0 us
  starting transfers between devices: 0.79 us -> 133 us
  matrix products: 536 us -> 450 us
  other arithmetic: 76.5 us -> 159 us
  local copies, waits for them, and re-layouts: 92.8 us -> 116 us
    all_gather x12 -> x4, waiting for transfers between devices: 551 us -> 14.1 us  [gather_weight(): return lax.all_gather(part, ('shard', 'group'), axis=0, tiled=True)]
    reduce_scatter x6 -> x0, waiting for transfers between devices: 435 us -> none  [the longest x2 179 us: one_batch(): lax.psum_scatter(tree_kv.astype(jnp.bfloat16), 'shard', scatter_dimension...]
    psum x2 -> x0, blocking collectives: 165 us -> none  [the longest x1 155 us: on_device(): lax.psum((h_qkv, h_out, h_fc1, h_b1, h_fc2, h_b2, h_ada, h_bada, h_gain1,...]
    ppermute x0 -> x80, starting transfers between devices: none -> 133 us  [the longest x24 42.8 us: turn(): return lax.ppermute(value, 'shard', [(i, (i + step) % n) for i in range(n)])]
    ppermute x0 -> x80, waiting for transfers between devices: none -> 119 us  [the longest x27 51.8 us: across(): lax.ppermute(value, 'group', [(i, i ^ 2 * step) for i in range(self.group...]
    convert_element_type x48 -> x33, other arithmetic: 31.8 us -> 126 us  [the longest x12 104 us: head_backward(): grad_score = (again * (grad_prob - delta_row)).astype(BF)]
    dot_general x196 -> x99, matrix products: 536 us -> 450 us  [the longest x40 207 us: mm_t(): lax.dot_general(left, right, (((1,), (1,)), ((), ())), preferred_element_...]
    while x236 -> x48, local copies, waits for them, and re-layouts: 54.4 us -> 0.09 us
  transfers between devices with their start and end apart: 19 -> 84, of which waited for: 16 -> 28; matrix products, arithmetic and copies ran while one was open for 15% -> 66% of each run, Pallas kernels for 0% -> 0%
where the time goes in v1:
time: 1020 us; the launch traced here: 1010 us
  matrix products  450 us (44%)
  other arithmetic  159 us (16%)
  starting transfers between devices  133 us (13%)
  waiting for transfers between devices  133 us (13%)
  local copies, waits for them, and re-layouts  116 us (11%)
  between operations  16.2 us (2%)
    dot_general x40, matrix products, mm_t(): lax.dot_general(left, right, (((1,), (1,)), ((), ())), preferred_element_...  207 us
    dot_general x28, matrix products, t_mm(): lax.dot_general(left, right, (((0,), (0,)), ((), ())), preferred_element_...  131 us
    dot_general x28, matrix products, mm(): return jnp.dot(left, right, preferred_element_type=F32)  109 us
    convert_element_type x12, other arithmetic, head_backward(): grad_score = (again * (grad_prob - delta_row)).astype(BF)  104 us
    ppermute x27, waiting for transfers between devices, across(): lax.ppermute(value, 'group', [(i, i ^ 2 * step) for i in range(self.group...  51.8 us
    ppermute x24, starting transfers between devices, turn(): return lax.ppermute(value, 'shard', [(i, (i + step) % n) for i in range(n)])  42.8 us
    unnamed x157, local copies, waits for them, and re-layouts  41.2 us
    ppermute x8, waiting for transfers between devices, to_trees(): got.append(lax.ppermute(piece, ('group', 'shard'), self.round_perm(k)))  37.3 us
  transfers between devices with their start and end apart: 84, of which 28 were waited for; matrix products, arithmetic and copies ran while one was open for 66% of the time, Pallas kernels for 0%

profile of v1, /device:TPU:1, one launch (start us, length us, event | category | flops | bytes accessed | tf_op | source)
XLA Modules:
  0.0 1008.4 jit_solution(8813397809625290388)
XLA Ops:
  38.3 10.6 %collective-permute-done.1 = bf16[256,768]{1,0:T(8,128)(2,1)S(1)} collective-permute-done((bf16[256,768]{1,0:T(8,128)(2,1)S(1)}, bf16[256,768]{1,0:T(8,128)(2,1)S(1)}, u32[]{:S(2)}, u32[]{:S(2)}) %collective-permute-start.1) | collective-permute-done | bytes 393248 | tf_op jit(solution)/shard_map/ppermute | solution.py:84
  48.9 9.2 collective-permute-done.2
  58.1 13.6 %collective-permute-done.3 = bf16[256,768]{1,0:T(8,128)(2,1)S(1)} collective-permute-done((bf16[256,768]{1,0:T(8,128)(2,1)S(1)}, bf16[256,768]{1,0:T(8,128)(2,1)S(1)}, u32[]{:S(2)}, u32[]{:S(2)}) %collective-permute-start.3) | collective-permute-done | bytes 393248 | tf_op jit(solution)/shard_map/ppermute | solution.py:84
  72.6 14.0 %all-gather.5.cloned.1.call-done = bf16[768,2304]{1,0:T(8,128)(2,1)} async-done(((bf16[24,2304]{1,0:T(8,128)(2,1)}), bf16[768,2304]{1,0:T(8,128)(2,1)}) %all-gather.5.cloned.1.call-update) | async-done | bytes 3538960 | tf_op jit(solution)/shard_map/all_gather | solution.py:112
  86.6 7.8 convolution_convert_fusion
  135.8 4.9 pad_maximum_fusion.2
  140.7 4.7 copy.75
  145.4 6.6 copy.78
  156.6 6.6 copy.79
  163.5 117.7 %while.28 = (s32[]{:T(128)}, bf16[12,1024,64]{1,2,0:T(8,128)(2,1)S(1)}, f32[12,1024,1]{1,2,0:T(1,128)}, bf16[12,1024,64]{2,1,0:T(8,128)(2,1)}, bf16[12,2048,64]{...) while((s32[]{:T(128)}, ...), condition=%wide.region_7.8_spmd.clone, body=%wide.region_4.7_spmd.clone.sunk | while | flops 564198400 | bytes 26671724 | solution.py:282
  288.0 15.2 %multiply_convert_fusion.1 = (bf16[1024,3072]{1,0:T(8,128)(2,1)}, f32[1024,3072]{1,0:T(8,128)}) fusion(f32[3072]{0:T(1024)S(1)} %copy-done.51, bf16[768,3072]{1,0:T(8,128)(2,1)} %all-gather.9.cloned.1.call-done, f32[1024,768]{1,0:T(8,128)} %copy-done.5, f32[768]{0:T(1024)S(1)} %copy-done.58, f32[768]{0:T(1024)S(1)} %get-tuple-element.449, ...), kind=kOutput, calls=%fused_computation.67 | convolution fusion | flops 4868014080 | bytes 26768384 | tf_op jit(solution)/shard_map/dot_general | solution.py:40
  303.4 18.2 %convert_reduce_fusion = (f32[3072]{0:T(1024)S(1)}, bf16[1024,3072]{1,0:T(8,128)(2,1)}) fusion(f32[1024,3072]{1,0:T(8,128)} %get-tuple-element.463, f32[3072]{0:T(1024)S(1)} %copy-done.51, bf16[3072,768]{1,0:T(8,128)(2,1)} %all-gather.11.cloned.1.call-done, f32[768]{0:T(1024)S(1)} %copy-done.55, bf16[256,768]{1,0:T(8,128)(2,1)} %collective-permute-done.16, ...), kind=kOutput, calls=%fused_computation.66 | convolution fusion | flops 4908905472 | bytes 25193472 | tf_op jit(solution)/shard_map/dot_general | solution.py:44
  321.6 7.5 fusion.145
  329.1 11.3 %convert_reduce_fusion.2 = (f32[768]{0:T(1024)S(1)}, f32[768]{0:T(1024)S(1)}, bf16[1024,768]{1,0:T(8,128)(2,1)}, f32[768]{0:T(1024)S(1)}, f32[1024]{0:T(1024)S(1...) fusion(f32[768]{0:T(1024)S(1)} %copy-done.55, bf16[256,768]{1,0:T(8,128)(2,1)} %collective-permute-done.16, ...), kind=kOutput, calls=%fused_computation.114 | convolution fusion | flops 4856210432 | bytes 20491264 | tf_op jit(solution)/shard_map/dot_general | solution.py:40
  356.9 7.7 convolution_convert_fusion.2
  370.6 372.0 %while.29 = (s32[]{:T(128)}, bf16[12,1024,64]{1,2,0:T(8,128)(2,1)S(1)}, f32[12,2048,64]{1,2,0:T(8,128)}, f32[12,2048,64]{1,2,0:T(8,128)}, bf16[12,1024,64]{2,1,0...) while((s32[]{:T(128)}, ...), condition=%wide.region_14.15_spmd.clone, body=%wide.region_12.14_spmd.clone.sunk | while | flops 1371798528 | bytes 117093568 | solution.py:326
  373.7 7.7 multiply_reduce_fusion.7
  381.4 8.6 multiply_convert_fusion.6
  393.9 5.2 fusion.196
  404.7 7.7 multiply_reduce_fusion.7
  412.3 8.6 multiply_convert_fusion.6
  424.9 5.2 fusion.196
  435.6 7.7 multiply_reduce_fusion.7
  443.3 8.6 multiply_convert_fusion.6
  455.9 5.2 fusion.196
  466.7 7.7 multiply_reduce_fusion.7
  474.3 8.6 multiply_convert_fusion.6
  486.9 5.2 fusion.196
  497.7 7.7 multiply_reduce_fusion.7
  505.4 8.6 multiply_convert_fusion.6
  517.9 5.2 fusion.196
  528.7 7.7 multiply_reduce_fusion.7
  536.4 8.6 multiply_convert_fusion.6
  548.9 5.2 fusion.196
  559.7 7.7 multiply_reduce_fusion.7
  567.3 8.6 multiply_convert_fusion.6
  579.9 5.2 fusion.196
  590.7 7.7 multiply_reduce_fusion.7
  598.3 8.6 multiply_convert_fusion.6
  610.9 5.2 fusion.196
  621.7 7.7 multiply_reduce_fusion.7
  629.3 8.6 multiply_convert_fusion.6
  641.9 5.2 fusion.196
  652.6 7.7 multiply_reduce_fusion.7
  660.3 8.6 multiply_convert_fusion.6
  672.9 5.2 fusion.196
  683.6 7.7 multiply_reduce_fusion.7
  691.3 8.6 multiply_convert_fusion.6
  703.8 5.2 fusion.196
  714.6 7.7 multiply_reduce_fusion.7
  722.3 8.6 multiply_convert_fusion.6
  734.9 5.2 fusion.196
  742.5 8.1 convolution_convert_fusion.1
  782.9 4.9 collective-permute-start.49
  787.8 8.7 collective-permute-done.48
  826.8 7.3 collective-permute-done.70
  838.4 8.5 collective-permute-done.72
  848.5 10.9 %collective-permute-done.56 = bf16[4,24,3072]{2,1,0:T(8,128)(2,1)S(1)} collective-permute-done((bf16[4,24,3072]{2,1,0:T(8,128)(2,1)S(1)}, bf16[4,24,3072]{2,1,0:T(8,128)(2,1)S(1)}, u32[]{:S(2)}, u32[]{:S(2)}) %collective-permute-start.56) | collective-permute-done | bytes 589856 | tf_op jit(solution)/shard_map/ppermute | solution.py:67
  861.3 11.9 %collective-permute-done.57 = bf16[4,24,3072]{2,1,0:T(8,128)(2,1)S(1)} collective-permute-done((bf16[4,24,3072]{2,1,0:T(8,128)(2,1)S(1)}, bf16[4,24,3072]{2,1,0:T(8,128)(2,1)S(1)}, u32[]{:S(2)}, u32[]{:S(2)}) %collective-permute-start.57) | collective-permute-done | bytes 589856 | tf_op jit(solution)/shard_map/ppermute | solution.py:67
  883.5 5.3 collective-permute-done.60
  891.3 5.2 fusion.74
  924.7 6.7 collective-permute-start.33
  938.4 5.1 collective-permute-start.19
  962.2 10.4 %collective-permute-start.79 = (bf16[384,768]{1,0:T(8,128)(2,1)S(1)}, bf16[384,768]{1,0:T(8,128)(2,1)S(1)}, u32[]{:S(2)}, u32[]{:S(2)}) collective-permute-start(bf16[384,768]{1,0:T(8,128)(2,1)S(1)} %bitcast.352), channel_id=1, source_target_pairs={{0,4},{4,0},{8,12},{12,8},{16,20},{20,16},{24,28},{28,24},{1,5},{5... | collective-permute-start | bytes 1769480 | tf_op jit(solution)/shard_map/ppermute | solution.py:60
  (642 shorter events, 502.3 us)
Async XLA Ops:
  7.2 79.4 %all-gather.5.cloned.1.call-start = ((), (), s32[]{:S(2)}) async-start(), calls=%async_computation | async-start | bytes 3649536 | tf_op jit(solution)/shard_map/all_gather | solution.py:112
  8.9 272.3 %all-gather.7.cloned.1.call-start = ((), (), s32[]{:S(2)}) async-start(), calls=%async_computation.1 | async-start | bytes 1216512 | tf_op jit(solution)/shard_map/all_gather | solution.py:112
  10.4 277.6 %all-gather.9.cloned.1.call-start = ((), (), s32[]{:S(2)}) async-start(), calls=%async_computation.2 | async-start | bytes 4866048 | tf_op jit(solution)/shard_map/all_gather | solution.py:112
  11.1 292.2 %all-gather.11.cloned.1.call-start = ((), (), s32[]{:S(2)}) async-start(), calls=%async_computation.3 | async-start | bytes 4866048 | tf_op jit(solution)/shard_map/all_gather | solution.py:112
  19.1 10.9 %collective-permute-start.5 = (f32[2496]{0:T(1024)S(1)}, f32[2496]{0:T(1024)S(1)}, u32[]{:S(2)}, u32[]{:S(2)}) collective-permute-start(f32[2496]{0:T(1024)S(1)} %get-tuple-element.301), channel_id=1, source_target_pairs={{0,1},{1,2},{2,3},{3,0},{4,5},{5,6},{6,7},{7,4},{8,9},{9,10},{10,1... | collective-permute-start | bytes 29960 | tf_op jit(solution)/shard_map/ppermute | solution.py:64
  21.8 10.0 collective-permute-start.6
  24.1 8.6 collective-permute-start.7
  26.7 11.6 %collective-permute-start = (bf16[256,768]{1,0:T(8,128)(2,1)S(1)}, bf16[256,768]{1,0:T(8,128)(2,1)S(1)}, u32[]{:S(2)}, u32[]{:S(2)}) collective-permute-start(bf16[256,768]{1,0:T(8,128)(2,1)S(1)} %get-tuple-element.387), channel_id=1, source_target_pairs={{0,0},{1,4},{2,2},{3,6},{4,1},{5,5},{6,3},{7,7},{8,8},{9,12},{10,1... | collective-permute-start | bytes 1179656 | tf_op jit(solution)/shard_map/ppermute | solution.py:84
  29.8 19.1 %collective-permute-start.1 = (bf16[256,768]{1,0:T(8,128)(2,1)S(1)}, bf16[256,768]{1,0:T(8,128)(2,1)S(1)}, u32[]{:S(2)}, u32[]{:S(2)}) collective-permute-start(bf16[256,768]{1,0:T(8,128)(2,1)S(1)} %get-tuple-element.390), channel_id=1, source_target_pairs={{0,4},{1,2},{2,6},{3,0},{4,5},{5,3},{6,7},{7,1},{8,12},{9,10},{10,... | collective-permute-start | bytes 1179656 | tf_op jit(solution)/shard_map/ppermute | solution.py:84
  29.9 28.1 %collective-permute-start.2 = (bf16[256,768]{1,0:T(8,128)(2,1)S(1)}, bf16[256,768]{1,0:T(8,128)(2,1)S(1)}, u32[]{:S(2)}, u32[]{:S(2)}) collective-permute-start(bf16[256,768]{1,0:T(8,128)(2,1)S(1)} %get-tuple-element.389), channel_id=1, source_target_pairs={{0,2},{1,6},{2,0},{3,4},{4,3},{5,7},{6,1},{7,5},{8,10},{9,14},{10,... | collective-permute-start | bytes 1179656 | tf_op jit(solution)/shard_map/ppermute | solution.py:84
  31.8 39.8 %collective-permute-start.3 = (bf16[256,768]{1,0:T(8,128)(2,1)S(1)}, bf16[256,768]{1,0:T(8,128)(2,1)S(1)}, u32[]{:S(2)}, u32[]{:S(2)}) collective-permute-start(bf16[256,768]{1,0:T(8,128)(2,1)S(1)} %get-tuple-element.388), channel_id=1, source_target_pairs={{0,6},{1,0},{2,4},{3,2},{4,7},{5,1},{6,5},{7,3},{8,14},{9,8},{10,1... | collective-permute-start | bytes 1179656 | tf_op jit(solution)/shard_map/ppermute | solution.py:84
  96.3 39.5 %collective-permute-start.8 = (bf16[1024,1536]{1,0:T(8,128)(2,1)}, bf16[1024,1536]{1,0:T(8,128)(2,1)}, u32[]{:S(2)}, u32[]{:S(2)}) collective-permute-start(bf16[1024,1536]{1,0:T(8,128)(2,1)} %slice.122), channel_id=1, source_target_pairs={{0,4},{4,0},{8,12},{12,8},{16,20},{20,16},{24,28},{28,24},{1,5},{5... | collective-permute-start | bytes 9437192 | tf_op jit(solution)/shard_map/ppermute | solution.py:60
  98.7 204.6 %collective-permute-start.13 = (bf16[256,768]{1,0:T(8,128)(2,1)}, bf16[256,768]{1,0:T(8,128)(2,1)S(1)}, u32[]{:S(2)}, u32[]{:S(2)}) collective-permute-start(bf16[256,768]{1,0:T(8,128)(2,1)} %get-tuple-element.379), channel_id=1, source_target_pairs={{0,0},{1,4},{2,2},{3,6},{4,1},{5,5},{6,3},{7,7},{8,8},{9,12},{10,1... | collective-permute-start | bytes 1179656 | tf_op jit(solution)/shard_map/ppermute | solution.py:84
  101.5 201.8 %collective-permute-start.14 = (bf16[256,768]{1,0:T(8,128)(2,1)}, bf16[256,768]{1,0:T(8,128)(2,1)}, u32[]{:S(2)}, u32[]{:S(2)}) collective-permute-start(bf16[256,768]{1,0:T(8,128)(2,1)} %get-tuple-element.382), channel_id=1, source_target_pairs={{0,4},{1,2},{2,6},{3,0},{4,5},{5,3},{6,7},{7,1},{8,12},{9,10},{10,... | collective-permute-start | bytes 1179656 | tf_op jit(solution)/shard_map/ppermute | solution.py:84
  101.6 201.7 %collective-permute-start.15 = (bf16[256,768]{1,0:T(8,128)(2,1)}, bf16[256,768]{1,0:T(8,128)(2,1)}, u32[]{:S(2)}, u32[]{:S(2)}) collective-permute-start(bf16[256,768]{1,0:T(8,128)(2,1)} %get-tuple-element.381), channel_id=1, source_target_pairs={{0,2},{1,6},{2,0},{3,4},{4,3},{5,7},{6,1},{7,5},{8,10},{9,14},{10,... | collective-permute-start | bytes 1179656 | tf_op jit(solution)/shard_map/ppermute | solution.py:84
  104.1 199.2 %collective-permute-start.16 = (bf16[256,768]{1,0:T(8,128)(2,1)}, bf16[256,768]{1,0:T(8,128)(2,1)}, u32[]{:S(2)}, u32[]{:S(2)}) collective-permute-start(bf16[256,768]{1,0:T(8,128)(2,1)} %get-tuple-element.380), channel_id=1, source_target_pairs={{0,6},{1,0},{2,4},{3,2},{4,7},{5,1},{6,5},{7,3},{8,14},{9,8},{10,1... | collective-permute-start | bytes 1179656 | tf_op jit(solution)/shard_map/ppermute | solution.py:84
  353.6 406.2 %collective-permute-start.26 = (f32[7680]{0:T(1024)}, f32[7680]{0:T(1024)S(1)}, u32[]{:S(2)}, u32[]{:S(2)}) collective-permute-start(f32[7680]{0:T(1024)} %constant_dynamic-update-slice_fusion.12), channel_id=1, source_target_pairs={{0,1},{1,2},{2,3},{3,0},{4,5},{5,6},{6,7},{7,4},{8,9},{9,10},{10,1... | collective-permute-start | bytes 92168 | tf_op jit(solution)/shard_map/ppermute | solution.py:64
  353.6 406.7 %collective-permute-start.27 = (f32[7680]{0:T(1024)}, f32[7680]{0:T(1024)S(1)}, u32[]{:S(2)}, u32[]{:S(2)}) collective-permute-start(f32[7680]{0:T(1024)} %constant_dynamic-update-slice_fusion.12), channel_id=1, source_target_pairs={{0,2},{1,3},{2,0},{3,1},{4,6},{5,7},{6,4},{7,5},{8,10},{9,11},{10,... | collective-permute-start | bytes 92168 | tf_op jit(solution)/shard_map/ppermute | solution.py:64
  354.1 408.1 %collective-permute-start.28 = (f32[7680]{0:T(1024)}, f32[7680]{0:T(1024)S(1)}, u32[]{:S(2)}, u32[]{:S(2)}) collective-permute-start(f32[7680]{0:T(1024)} %constant_dynamic-update-slice_fusion.12), channel_id=1, source_target_pairs={{0,3},{1,0},{2,1},{3,2},{4,7},{5,4},{6,5},{7,6},{8,11},{9,8},{10,9... | collective-permute-start | bytes 92168 | tf_op jit(solution)/shard_map/ppermute | solution.py:64
  752.2 64.9 %collective-permute-start.69 = (bf16[4,384,768]{2,1,0:T(8,128)(2,1)}, bf16[4,384,768]{2,1,0:T(8,128)(2,1)}, u32[]{:S(2)}, u32[]{:S(2)}) collective-permute-start(bf16[4,384,768]{2,1,0:T(8,128)(2,1)} %dynamic-slice_bitcast_fusion), channel_id=1, source_target_pairs={{0,4},{4,0},{8,12},{12,8},{16,20},{20,16},{24,28},{28,24},{1,5},{5... | collective-permute-start | bytes 7077896 | tf_op jit(solution)/shard_map/ppermute | solution.py:60
  757.0 63.1 %collective-permute-start.55 = (bf16[4,96,3072]{2,1,0:T(8,128)(2,1)}, bf16[4,96,3072]{2,1,0:T(8,128)(2,1)S(1)}, u32[]{:S(2)}, u32[]{:S(2)}) collective-permute-start(bf16[4,96,3072]{2,1,0:T(8,128)(2,1)} %dynamic-slice_bitcast_fusion.1), channel_id=1, source_target_pairs={{0,4},{4,0},{8,12},{12,8},{16,20},{20,16},{24,28},{28,24},{1,5},{5... | collective-permute-start | bytes 7077896 | tf_op jit(solution)/shard_map/ppermute | solution.py:60
  760.3 21.1 %collective-permute-start.9 = (bf16[256,768]{1,0:T(8,128)(2,1)}, bf16[256,768]{1,0:T(8,128)(2,1)}, u32[]{:S(2)}, u32[]{:S(2)}) collective-permute-start(bf16[256,768]{1,0:T(8,128)(2,1)} %get-tuple-element.386), channel_id=1, source_target_pairs={{0,0},{4,1},{2,2},{6,3},{1,4},{5,5},{3,6},{7,7},{8,8},{12,9},{10,1... | collective-permute-start | bytes 1179656 | tf_op jit(solution)/shard_map/ppermute | solution.py:93
  779.4 26.2 %collective-permute-start.11 = (bf16[256,768]{1,0:T(8,128)(2,1)}, bf16[256,768]{1,0:T(8,128)(2,1)S(1)}, u32[]{:S(2)}, u32[]{:S(2)}) collective-permute-start(bf16[256,768]{1,0:T(8,128)(2,1)} %get-tuple-element.384), channel_id=1, source_target_pairs={{2,0},{6,1},{0,2},{4,3},{3,4},{7,5},{1,6},{5,7},{10,8},{14,9},{8,1... | collective-permute-start | bytes 1179656 | tf_op jit(solution)/shard_map/ppermute | solution.py:93
  781.4 15.1 %collective-permute-start.48 = (bf16[24,768]{1,0:T(8,128)(2,1)S(1)}, bf16[24,768]{1,0:T(8,128)(2,1)S(1)}, u32[]{:S(2)}, u32[]{:S(2)}) collective-permute-start(bf16[24,768]{1,0:T(8,128)(2,1)S(1)} %get-tuple-element.423), channel_id=1, source_target_pairs={{0,1},{1,2},{2,3},{3,0},{4,5},{5,6},{6,7},{7,4},{8,9},{9,10},{10,1... | collective-permute-start | bytes 110600 | tf_op jit(solution)/shard_map/ppermute | solution.py:64
  782.9 20.8 %collective-permute-start.49 = (bf16[24,768]{1,0:T(8,128)(2,1)S(1)}, bf16[24,768]{1,0:T(8,128)(2,1)S(1)}, u32[]{:S(2)}, u32[]{:S(2)}) collective-permute-start(bf16[24,768]{1,0:T(8,128)(2,1)S(1)} %get-tuple-element.425), channel_id=1, source_target_pairs={{0,2},{1,3},{2,0},{3,1},{4,6},{5,7},{6,4},{7,5},{8,10},{9,11},{10,... | collective-permute-start | bytes 110600 | tf_op jit(solution)/shard_map/ppermute | solution.py:64
  796.5 7.6 collective-permute-start.50
  805.3 7.3 collective-permute-start.52
  805.6 11.3 %collective-permute-start.53 = (bf16[24,768]{1,0:T(8,128)(2,1)S(1)}, bf16[24,768]{1,0:T(8,128)(2,1)S(1)}, u32[]{:S(2)}, u32[]{:S(2)}) collective-permute-start(bf16[24,768]{1,0:T(8,128)(2,1)S(1)} %fusion.118), channel_id=1, source_target_pairs={{0,24},{4,28},{8,16},{12,20},{16,8},{20,12},{24,0},{28,4},{1,25},{... | collective-permute-start | bytes 110600 | tf_op jit(solution)/shard_map/ppermute | solution.py:67
  808.0 80.9 %collective-permute-start.17 = (bf16[1024,1536]{0,1:T(8,128)(2,1)S(1)}, bf16[1024,1536]{0,1:T(8,128)(2,1)S(1)}, u32[]{:S(2)}, u32[]{:S(2)}) collective-permute-start(bf16[1024,1536]{0,1:T(8,128)(2,1)S(1)} %fusion.60), channel_id=1, source_target_pairs={{0,4},{4,0},{8,12},{12,8},{16,20},{20,16},{24,28},{28,24},{1,5},{5... | collective-permute-start | bytes 9437192 | tf_op jit(solution)/shard_map/ppermute | solution.py:60
  812.7 12.3 %collective-permute-start.12 = (bf16[256,768]{1,0:T(8,128)(2,1)S(1)}, bf16[256,768]{1,0:T(8,128)(2,1)S(1)}, u32[]{:S(2)}, u32[]{:S(2)}) collective-permute-start(bf16[256,768]{1,0:T(8,128)(2,1)S(1)} %copy-done.29), channel_id=1, source_target_pairs={{6,0},{0,1},{4,2},{2,3},{7,4},{1,5},{5,6},{3,7},{14,8},{8,9},{12,1... | collective-permute-start | bytes 1179656 | tf_op jit(solution)/shard_map/ppermute | solution.py:93
  817.0 9.2 collective-permute-start.54
  819.5 14.5 %collective-permute-start.70 = (bf16[4,96,768]{2,1,0:T(8,128)(2,1)S(1)}, bf16[4,96,768]{2,1,0:T(8,128)(2,1)S(1)}, u32[]{:S(2)}, u32[]{:S(2)}) collective-permute-start(bf16[4,96,768]{2,1,0:T(8,128)(2,1)S(1)} %get-tuple-element.366), channel_id=1, source_target_pairs={{0,8},{4,12},{8,0},{12,4},{16,24},{20,28},{24,16},{28,20},{1,9},{5... | collective-permute-start | bytes 1769480 | tf_op jit(solution)/shard_map/ppermute | solution.py:67
  820.1 14.4 %collective-permute-start.71 = (bf16[4,96,768]{2,1,0:T(8,128)(2,1)S(1)}, bf16[4,96,768]{2,1,0:T(8,128)(2,1)S(1)}, u32[]{:S(2)}, u32[]{:S(2)}) collective-permute-start(bf16[4,96,768]{2,1,0:T(8,128)(2,1)S(1)} %get-tuple-element.368), channel_id=1, source_target_pairs={{0,16},{4,20},{8,24},{12,28},{16,0},{20,4},{24,8},{28,12},{1,17},{... | collective-permute-start | bytes 1769480 | tf_op jit(solution)/shard_map/ppermute | solution.py:67
  825.0 22.0 %collective-permute-start.72 = (bf16[4,96,768]{2,1,0:T(8,128)(2,1)S(1)}, bf16[4,96,768]{2,1,0:T(8,128)(2,1)S(1)}, u32[]{:S(2)}, u32[]{:S(2)}) collective-permute-start(bf16[4,96,768]{2,1,0:T(8,128)(2,1)S(1)} %get-tuple-element.367), channel_id=1, source_target_pairs={{0,24},{4,28},{8,16},{12,20},{16,8},{20,12},{24,0},{28,4},{1,25},{... | collective-permute-start | bytes 1769480 | tf_op jit(solution)/shard_map/ppermute | solution.py:67
  826.2 33.2 %collective-permute-start.56 = (bf16[4,24,3072]{2,1,0:T(8,128)(2,1)S(1)}, bf16[4,24,3072]{2,1,0:T(8,128)(2,1)S(1)}, u32[]{:S(2)}, u32[]{:S(2)}) collective-permute-start(bf16[4,24,3072]{2,1,0:T(8,128)(2,1)S(1)} %get-tuple-element.369), channel_id=1, source_target_pairs={{0,8},{4,12},{8,0},{12,4},{16,24},{20,28},{24,16},{28,20},{1,9},{5... | collective-permute-start | bytes 1769480 | tf_op jit(solution)/shard_map/ppermute | solution.py:67
  834.1 39.1 %collective-permute-start.57 = (bf16[4,24,3072]{2,1,0:T(8,128)(2,1)S(1)}, bf16[4,24,3072]{2,1,0:T(8,128)(2,1)S(1)}, u32[]{:S(2)}, u32[]{:S(2)}) collective-permute-start(bf16[4,24,3072]{2,1,0:T(8,128)(2,1)S(1)} %get-tuple-element.371), channel_id=1, source_target_pairs={{0,16},{4,20},{8,24},{12,28},{16,0},{20,4},{24,8},{28,12},{1,17},{... | collective-permute-start | bytes 1769480 | tf_op jit(solution)/shard_map/ppermute | solution.py:67
  834.5 40.1 %collective-permute-start.58 = (bf16[4,24,3072]{2,1,0:T(8,128)(2,1)S(1)}, bf16[4,24,3072]{2,1,0:T(8,128)(2,1)S(1)}, u32[]{:S(2)}, u32[]{:S(2)}) collective-permute-start(bf16[4,24,3072]{2,1,0:T(8,128)(2,1)S(1)} %get-tuple-element.370), channel_id=1, source_target_pairs={{0,24},{4,28},{8,16},{12,20},{16,8},{20,12},{24,0},{28,4},{1,25},{... | collective-permute-start | bytes 1769480 | tf_op jit(solution)/shard_map/ppermute | solution.py:67
  847.3 27.9 %collective-permute-start.73 = (bf16[96,768]{1,0:T(8,128)(2,1)S(1)}, bf16[96,768]{1,0:T(8,128)(2,1)S(1)}, u32[]{:S(2)}, u32[]{:S(2)}) collective-permute-start(bf16[96,768]{1,0:T(8,128)(2,1)S(1)} %get-tuple-element.399), channel_id=1, source_target_pairs={{0,1},{1,2},{2,3},{3,0},{4,5},{5,6},{6,7},{7,4},{8,9},{9,10},{10,1... | collective-permute-start | bytes 442376 | tf_op jit(solution)/shard_map/ppermute | solution.py:64
  859.4 18.0 %collective-permute-start.74 = (bf16[96,768]{1,0:T(8,128)(2,1)S(1)}, bf16[96,768]{1,0:T(8,128)(2,1)S(1)}, u32[]{:S(2)}, u32[]{:S(2)}) collective-permute-start(bf16[96,768]{1,0:T(8,128)(2,1)S(1)} %get-tuple-element.401), channel_id=1, source_target_pairs={{0,2},{1,3},{2,0},{3,1},{4,6},{5,7},{6,4},{7,5},{8,10},{9,11},{10,... | collective-permute-start | bytes 442376 | tf_op jit(solution)/shard_map/ppermute | solution.py:64
  875.0 8.3 collective-permute-start.59
  875.1 13.6 %collective-permute-start.60 = (bf16[24,3072]{1,0:T(8,128)(2,1)S(1)}, bf16[24,3072]{1,0:T(8,128)(2,1)S(1)}, u32[]{:S(2)}, u32[]{:S(2)}) collective-permute-start(bf16[24,3072]{1,0:T(8,128)(2,1)S(1)} %get-tuple-element.408), channel_id=1, source_target_pairs={{0,2},{1,3},{2,0},{3,1},{4,6},{5,7},{6,4},{7,5},{8,10},{9,11},{10,... | collective-permute-start | bytes 442376 | tf_op jit(solution)/shard_map/ppermute | solution.py:64
  877.4 11.4 %collective-permute-start.61 = (bf16[24,3072]{1,0:T(8,128)(2,1)S(1)}, bf16[24,3072]{1,0:T(8,128)(2,1)S(1)}, u32[]{:S(2)}, u32[]{:S(2)}) collective-permute-start(bf16[24,3072]{1,0:T(8,128)(2,1)S(1)} %get-tuple-element.407), channel_id=1, source_target_pairs={{0,3},{1,0},{2,1},{3,2},{4,7},{5,4},{6,5},{7,6},{8,11},{9,8},{10,9... | collective-permute-start | bytes 442376 | tf_op jit(solution)/shard_map/ppermute | solution.py:64
  878.4 55.0 %collective-permute-start.76 = (bf16[96,768]{1,0:T(8,128)(2,1)S(1)}, bf16[96,768]{1,0:T(8,128)(2,1)S(1)}, u32[]{:S(2)}, u32[]{:S(2)}) collective-permute-start(bf16[96,768]{1,0:T(8,128)(2,1)S(1)} %fusion.106), channel_id=1, source_target_pairs={{0,8},{4,12},{8,0},{12,4},{16,24},{20,28},{24,16},{28,20},{1,9},{5... | collective-permute-start | bytes 442376 | tf_op jit(solution)/shard_map/ppermute | solution.py:67
  883.3 52.4 %collective-permute-start.77 = (bf16[96,768]{1,0:T(8,128)(2,1)S(1)}, bf16[96,768]{1,0:T(8,128)(2,1)S(1)}, u32[]{:S(2)}, u32[]{:S(2)}) collective-permute-start(bf16[96,768]{1,0:T(8,128)(2,1)S(1)} %fusion.106), channel_id=1, source_target_pairs={{0,16},{4,20},{8,24},{12,28},{16,0},{20,4},{24,8},{28,12},{1,17},{... | collective-permute-start | bytes 442376 | tf_op jit(solution)/shard_map/ppermute | solution.py:67
  896.6 15.3 %collective-permute-start.22 = (f32[2304]{0:T(1024)S(1)}, f32[2304]{0:T(1024)S(1)}, u32[]{:S(2)}, u32[]{:S(2)}) collective-permute-start(f32[2304]{0:T(1024)S(1)} %pad_maximum_fusion.27), channel_id=1, source_target_pairs={{0,1},{1,2},{2,3},{3,0},{4,5},{5,6},{6,7},{7,4},{8,9},{9,10},{10,1... | collective-permute-start | bytes 27656 | tf_op jit(solution)/shard_map/ppermute | solution.py:64
  900.1 11.8 %collective-permute-start.23 = (f32[2304]{0:T(1024)S(1)}, f32[2304]{0:T(1024)S(1)}, u32[]{:S(2)}, u32[]{:S(2)}) collective-permute-start(f32[2304]{0:T(1024)S(1)} %pad_maximum_fusion.27), channel_id=1, source_target_pairs={{0,2},{1,3},{2,0},{3,1},{4,6},{5,7},{6,4},{7,5},{8,10},{9,11},{10,... | collective-permute-start | bytes 27656 | tf_op jit(solution)/shard_map/ppermute | solution.py:64
  903.0 8.9 collective-permute-start.24
  920.5 10.9 %collective-permute-start.64 = (bf16[24,3072]{1,0:T(8,128)(2,1)S(1)}, bf16[24,3072]{1,0:T(8,128)(2,1)S(1)}, u32[]{:S(2)}, u32[]{:S(2)}) collective-permute-start(bf16[24,3072]{1,0:T(8,128)(2,1)S(1)} %fusion.109), channel_id=1, source_target_pairs={{0,24},{4,28},{8,16},{12,20},{16,8},{20,12},{24,0},{28,4},{1,25},{... | collective-permute-start | bytes 442376 | tf_op jit(solution)/shard_map/ppermute | solution.py:67
  923.1 12.7 %collective-permute-start.78 = (bf16[96,768]{1,0:T(8,128)(2,1)S(1)}, bf16[96,768]{1,0:T(8,128)(2,1)S(1)}, u32[]{:S(2)}, u32[]{:S(2)}) collective-permute-start(bf16[96,768]{1,0:T(8,128)(2,1)S(1)} %fusion.106), channel_id=1, source_target_pairs={{0,24},{4,28},{8,16},{12,20},{16,8},{20,12},{24,0},{28,4},{1,25},{... | collective-permute-start | bytes 442376 | tf_op jit(solution)/shard_map/ppermute | solution.py:67
  924.7 25.4 %collective-permute-start.33 = (bf16[4,96,2304]{2,1,0:T(8,128)(2,1)}, bf16[4,96,2304]{2,1,0:T(8,128)(2,1)}, u32[]{:S(2)}, u32[]{:S(2)}) collective-permute-start(bf16[4,96,2304]{2,1,0:T(8,128)(2,1)} %dynamic-slice_bitcast_fusion.2), channel_id=1, source_target_pairs={{0,4},{4,0},{8,12},{12,8},{16,20},{20,16},{24,28},{28,24},{1,5},{5... | collective-permute-start | bytes 5308424 | tf_op jit(solution)/shard_map/ppermute | solution.py:60
  931.4 23.3 %collective-permute-start.18 = (bf16[256,768]{1,0:T(8,128)(2,1)}, bf16[256,768]{1,0:T(8,128)(2,1)}, u32[]{:S(2)}, u32[]{:S(2)}) collective-permute-start(bf16[256,768]{1,0:T(8,128)(2,1)} %get-tuple-element.378), channel_id=1, source_target_pairs={{0,0},{4,1},{2,2},{6,3},{1,4},{5,5},{3,6},{7,7},{8,8},{12,9},{10,1... | collective-permute-start | bytes 1179656 | tf_op jit(solution)/shard_map/ppermute | solution.py:93
  935.7 7.8 collective-permute-start.67
  935.8 9.0 collective-permute-start.68
  938.4 18.6 %collective-permute-start.19 = (bf16[256,768]{1,0:T(8,128)(2,1)}, bf16[256,768]{1,0:T(8,128)(2,1)}, u32[]{:S(2)}, u32[]{:S(2)}) collective-permute-start(bf16[256,768]{1,0:T(8,128)(2,1)} %get-tuple-element.377), channel_id=1, source_target_pairs={{4,0},{2,1},{6,2},{0,3},{5,4},{3,5},{7,6},{1,7},{12,8},{10,9},{14,... | collective-permute-start | bytes 1179656 | tf_op jit(solution)/shard_map/ppermute | solution.py:93
  943.4 35.1 %collective-permute-start.20 = (bf16[256,768]{1,0:T(8,128)(2,1)S(1)}, bf16[256,768]{1,0:T(8,128)(2,1)}, u32[]{:S(2)}, u32[]{:S(2)}) collective-permute-start(bf16[256,768]{1,0:T(8,128)(2,1)S(1)} %get-tuple-element.376), channel_id=1, source_target_pairs={{2,0},{6,1},{0,2},{4,3},{3,4},{7,5},{1,6},{5,7},{10,8},{14,9},{8,1... | collective-permute-start | bytes 1179656 | tf_op jit(solution)/shard_map/ppermute | solution.py:93
  952.6 9.6 collective-permute-start.34
  954.6 18.1 %collective-permute-start.35 = (bf16[4,24,2304]{2,1,0:T(8,128)(2,1)S(1)}, bf16[4,24,2304]{2,1,0:T(8,128)(2,1)S(1)}, u32[]{:S(2)}, u32[]{:S(2)}) collective-permute-start(bf16[4,24,2304]{2,1,0:T(8,128)(2,1)S(1)} %get-tuple-element.374), channel_id=1, source_target_pairs={{0,16},{4,20},{8,24},{12,28},{16,0},{20,4},{24,8},{28,12},{1,17},{... | collective-permute-start | bytes 1327112 | tf_op jit(solution)/shard_map/ppermute | solution.py:67
  954.7 18.9 %collective-permute-start.36 = (bf16[4,24,2304]{2,1,0:T(8,128)(2,1)S(1)}, bf16[4,24,2304]{2,1,0:T(8,128)(2,1)S(1)}, u32[]{:S(2)}, u32[]{:S(2)}) collective-permute-start(bf16[4,24,2304]{2,1,0:T(8,128)(2,1)S(1)} %get-tuple-element.373), channel_id=1, source_target_pairs={{0,24},{4,28},{8,16},{12,20},{16,8},{20,12},{24,0},{28,4},{1,25},{... | collective-permute-start | bytes 1327112 | tf_op jit(solution)/shard_map/ppermute | solution.py:67
  957.0 32.4 %collective-permute-start.21 = (bf16[256,768]{1,0:T(8,128)(2,1)S(1)}, bf16[256,768]{1,0:T(8,128)(2,1)S(1)}, u32[]{:S(2)}, u32[]{:S(2)}) collective-permute-start(bf16[256,768]{1,0:T(8,128)(2,1)S(1)} %get-tuple-element.375), channel_id=1, source_target_pairs={{6,0},{0,1},{4,2},{2,3},{7,4},{1,5},{5,6},{3,7},{14,8},{8,9},{12,1... | collective-permute-start | bytes 1179656 | tf_op jit(solution)/shard_map/ppermute | solution.py:93
  962.2 34.8 %collective-permute-start.79 = (bf16[384,768]{1,0:T(8,128)(2,1)S(1)}, bf16[384,768]{1,0:T(8,128)(2,1)S(1)}, u32[]{:S(2)}, u32[]{:S(2)}) collective-permute-start(bf16[384,768]{1,0:T(8,128)(2,1)S(1)} %bitcast.352), channel_id=1, source_target_pairs={{0,4},{4,0},{8,12},{12,8},{16,20},{20,16},{24,28},{28,24},{1,5},{5... | collective-permute-start | bytes 1769480 | tf_op jit(solution)/shard_map/ppermute | solution.py:60
  973.8 8.0 collective-permute-start.37
  978.4 9.4 collective-permute-start.38
  978.5 9.2 collective-permute-start.39
  981.9 16.8 %collective-permute-start.65 = (bf16[96,3072]{1,0:T(8,128)(2,1)S(1)}, bf16[96,3072]{1,0:T(8,128)(2,1)S(1)}, u32[]{:S(2)}, u32[]{:S(2)}) collective-permute-start(bf16[96,3072]{1,0:T(8,128)(2,1)S(1)} %bitcast.350), channel_id=1, source_target_pairs={{0,4},{4,0},{8,12},{12,8},{16,20},{20,16},{24,28},{28,24},{1,5},{5... | collective-permute-start | bytes 1769480 | tf_op jit(solution)/shard_map/ppermute | solution.py:60
  (116 other events, 3259.2 us)
Sparse Core Ops, SparseCore 0:
  11.5 75.0 all-gather.4
  89.5 63.1 all-gather.6
  156.2 62.6 all-gather.8
  222.2 62.4 all-gather.10

commit v2 on v1

--- a/solution.py
+++ b/solution.py
@@ -1,8 +1,11 @@
+import functools
 import math
 
 import jax
 import jax.numpy as jnp
 from jax import lax
+from jax.experimental import pallas as pl
+from jax.experimental.pallas import tpu as pltpu
 from jax.sharding import PartitionSpec as P
 
 HEADS = 12
@@ -12,6 +15,11 @@
 HIGH = lax.Precision.HIGHEST
 BF = jnp.bfloat16
 F32 = jnp.float32
+BLOCK = 256
+LANES = 128
+BIG = -float(2**30)
+MASKED = -1000000000.0
+PAIRS = 6
 
 
 def layer_norm(values):
@@ -46,6 +54,212 @@
 
 def t_mm(left, right):
     return lax.dot_general(left, right, (((0,), (0,)), ((), ())), preferred_element_type=F32)
+
+
+def split_heads(pair):
+    first = lax.broadcasted_iota(jnp.int32, pair.shape, 1) < LANES // 2
+    zero = jnp.zeros_like(pair)
+    return jnp.concatenate([jnp.where(first, pair, zero), jnp.where(first, zero, pair)], axis=0)
+
+def side_by_side(stack):
+    n = stack.shape[0] // 2
+    return jnp.concatenate([stack[:n], stack[n:]], axis=1)
+
+def lanes_sum(x): return jnp.sum(x, axis=1, keepdims=True)
+
+def fwd_kernel(near, pp, scale, flags, q_ref, kn_ref, vn_ref, kf_ref, vf_ref, feat_ref, hot_ref, o_ref, lse_ref,
+               s_ref, m_ref, l_ref, acc_ref, k_all, v_all):
+    qb = pl.program_id(1)
+    nk = hot_ref.shape[0] // BLOCK
+    safe = flags[flags.shape[0] - 1] == 1
+    @pl.when(qb == 0)
+    def _():
+        k_all[:near] = kn_ref[...]; k_all[near:] = kf_ref[...]
+        v_all[:near] = vn_ref[...]; v_all[near:] = vf_ref[...]
+    feat = feat_ref[...]
+    feat2 = jnp.concatenate([feat, feat], axis=0)
+    qs = [split_heads(q_ref[:, p*LANES:(p+1)*LANES] * scale) for p in range(pp)]
+    m_ref[...] = jnp.full(m_ref.shape, -jnp.inf, F32)
+    def scan_scores(exact):
+        def step(j, _):
+            @pl.when(flags[qb * nk + j] == 1)
+            def _():
+                rows = pl.ds(pl.multiple_of(j * BLOCK, BLOCK), BLOCK)
+                hot = hot_ref[rows, :]
+                for p in range(pp):
+                    k = k_all[rows, p*LANES:(p+1)*LANES]
+                    if exact:
+                        ok = mm_t(feat2, hot) > -1.0
+                        s = jnp.where(ok, mm_t(qs[p], k), MASKED)
+                    else:
+                        s = mm_t(jnp.concatenate([qs[p], feat2], axis=1), jnp.concatenate([k, hot], axis=1))
+                    s_ref[p, j] = s
+                    m_ref[p] = jnp.maximum(m_ref[p], jnp.maximum(s[:, :LANES], s[:, LANES:]))
+            return 0
+        lax.fori_loop(0, nk, step, 0)
+    @pl.when(safe)
+    def _(): scan_scores(False)
+    @pl.when(jnp.logical_not(safe))
+    def _(): scan_scores(True)
+    tops = [jnp.max(m_ref[p], axis=1, keepdims=True) for p in range(pp)]
+    l_ref[...] = jnp.zeros(l_ref.shape, F32)
+    acc_ref[...] = jnp.zeros(acc_ref.shape, F32)
+    def step(j, _):
+        @pl.when(flags[qb * nk + j] == 1)
+        def _():
+            rows = pl.ds(pl.multiple_of(j * BLOCK, BLOCK), BLOCK)
+            for p in range(pp):
+                e = jnp.exp(s_ref[p, j] - tops[p])
+                l_ref[p] += e[:, :LANES] + e[:, LANES:]
+                v = split_heads(v_all[rows, p*LANES:(p+1)*LANES])
+                acc_ref[p] += mm(side_by_side(e.astype(BF)), v)
+        return 0
+    lax.fori_loop(0, nk, step, 0)
+    for p in range(pp):
+        total = lanes_sum(l_ref[p])
+        lse_ref[p, 0] = tops[p] + jnp.log(total)
+        first = lax.broadcasted_iota(jnp.int32, (BLOCK, LANES), 1) < LANES // 2
+        o_ref[:, p*LANES:(p+1)*LANES] = (acc_ref[p] / jnp.where(first, total[:BLOCK], total[BLOCK:])).astype(BF)
+
+def attn_fwd(q, kv, far, feat, hot, flags, scale, pp):
+    near, width = q.shape
+    total = hot.shape[0]
+    steps = width // LANES // pp
+    nq = near // BLOCK
+    col = lambda c: (lambda h, i, f: (0, c * steps + h))
+    return pl.pallas_call(
+        functools.partial(fwd_kernel, near, pp, scale),
+        grid_spec=pltpu.PrefetchScalarGridSpec(
+            num_scalar_prefetch=1, grid=(steps, nq),
+            in_specs=[
+                pl.BlockSpec((BLOCK, pp*LANES), lambda h, i, f: (i, h)),
+                pl.BlockSpec((near, pp*LANES), col(0)),
+                pl.BlockSpec((near, pp*LANES), col(1)),
+                pl.BlockSpec((near, pp*LANES), col(0)),
+                pl.BlockSpec((near, pp*LANES), col(1)),
+                pl.BlockSpec((BLOCK, LANES), lambda h, i, f: (i, 0)),
+                pl.BlockSpec((total, LANES), lambda h, i, f: (0, 0)),
+            ],
+            out_specs=[
+                pl.BlockSpec((BLOCK, pp*LANES), lambda h, i, f: (i, h)),
+                pl.BlockSpec((pp, 1, 2*BLOCK, 1), lambda h, i, f: (h, i, 0, 0)),
+            ],
+            scratch_shapes=[
+                pltpu.VMEM((pp, total // BLOCK, 2*BLOCK, BLOCK), F32),
+                pltpu.VMEM((pp, 2*BLOCK, LANES), F32),
+                pltpu.VMEM((pp, 2*BLOCK, LANES), F32),
+                pltpu.VMEM((pp, BLOCK, LANES), F32),
+                pltpu.VMEM((total, pp*LANES), BF),
+                pltpu.VMEM((total, pp*LANES), BF),
+            ]),
+        out_shape=[jax.ShapeDtypeStruct((near, width), BF), jax.ShapeDtypeStruct((width // LANES, nq, 2*BLOCK, 1), F32)],
+        compiler_params=pltpu.CompilerParams(vmem_limit_bytes=56<<20),
+        cost_estimate=pl.CostEstimate(flops=4*near*total*width, bytes_accessed=8*near*width*2, transcendentals=near*total*width//64),
+        name="attn_forward",
+    )(flags, q, kv, kv, far, far, feat, hot)
+
+def bwd_kernel(near, pp, scale, flags, q_ref, kn_ref, vn_ref, kf_ref, vf_ref, feat_ref, hot_ref, o_ref, do_ref, lse_ref,
+               dq_ref, near_ref, far_ref, k_all, v_all, dk_acc, dv_acc, dq_acc):
+    qb = pl.program_id(1)
+    nk = hot_ref.shape[0] // BLOCK
+    safe = flags[flags.shape[0] - 1] == 1
+    @pl.when(qb == 0)
+    def _():
+        k_all[:near] = kn_ref[...]; k_all[near:] = kf_ref[...]
+        v_all[:near] = vn_ref[...]; v_all[near:] = vf_ref[...]
+        dk_acc[...] = jnp.zeros(dk_acc.shape, F32)
+        dv_acc[...] = jnp.zeros(dv_acc.shape, F32)
+    feat = feat_ref[...]
+    feat2 = jnp.concatenate([feat, feat], axis=0)
+    dq_acc[...] = jnp.zeros(dq_acc.shape, F32)
+    qs, dos, deltas, lses = [], [], [], []
+    for p in range(pp):
+        cols = slice(p*LANES, (p+1)*LANES)
+        qs.append(split_heads(q_ref[:, cols] * scale))
+        do2 = split_heads(do_ref[:, cols])
+        dos.append(do2)
+        o = o_ref[:, cols].astype(F32)
+        deltas.append(lanes_sum(do2.astype(F32) * jnp.concatenate([o, o], axis=0)))
+        lses.append(lse_ref[p, 0])
+    def sweep(exact):
+        def step(j, _):
+            @pl.when(flags[qb * nk + j] == 1)
+            def _():
+                rows = pl.ds(pl.multiple_of(j * BLOCK, BLOCK), BLOCK)
+                hot = hot_ref[rows, :]
+                for p in range(pp):
+                    cols = slice(p*LANES, (p+1)*LANES)
+                    k = k_all[rows, cols]; v = v_all[rows, cols]
+                    if exact:
+                        ok = mm_t(feat2, hot) > -1.0
+                        s = jnp.where(ok, mm_t(qs[p], k), MASKED)
+                    else:
+                        s = mm_t(jnp.concatenate([qs[p], feat2], axis=1), jnp.concatenate([k, hot], axis=1))
+                    prob = jnp.exp(s - lses[p])
+                    dprob = mm_t(dos[p], v)
+                    ds = prob * (dprob - deltas[p])
+                    if exact:
+                        ds = jnp.where(ok, ds, 0.0)
+                    ds = ds.astype(BF)
+                    dv_acc[rows, cols] += t_mm(prob.astype(BF), dos[p])
+                    dk_acc[rows, cols] += t_mm(ds, qs[p])
+                    dq_acc[p] += mm(side_by_side(ds), split_heads(k))
+            return 0
+        lax.fori_loop(0, nk, step, 0)
+    @pl.when(safe)
+    def _(): sweep(False)
+    @pl.when(jnp.logical_not(safe))
+    def _(): sweep(True)
+    for p in range(pp):
+        dq_ref[:, p*LANES:(p+1)*LANES] = (dq_acc[p] * scale).astype(BF)
+    @pl.when(qb == pl.num_programs(1) - 1)
+    def _():
+        near_ref[0] = dk_acc[:near]
+        near_ref[1] = dv_acc[:near]
+        far_ref[0] = dk_acc[near:].astype(BF)
+        far_ref[1] = dv_acc[near:].astype(BF)
+
+def attn_bwd(q, kv, far, feat, hot, flags, attn, dattn, lse, scale, pp):
+    near, width = q.shape
+    total = hot.shape[0]
+    steps = width // LANES // pp
+    nq = near // BLOCK
+    col = lambda c: (lambda h, i, f: (0, c * steps + h))
+    rowblk = pl.BlockSpec((BLOCK, pp*LANES), lambda h, i, f: (i, h))
+    whole = pl.BlockSpec((near, pp*LANES), col(0))
+    both = pl.BlockSpec((2, near, pp*LANES), lambda h, i, f: (0, 0, h))
+    return pl.pallas_call(
+        functools.partial(bwd_kernel, near, pp, scale),
+        grid_spec=pltpu.PrefetchScalarGridSpec(
+            num_scalar_prefetch=1, grid=(steps, nq),
+            in_specs=[
+                rowblk,
+                pl.BlockSpec((near, pp*LANES), col(0)),
+                pl.BlockSpec((near, pp*LANES), col(1)),
+                whole,
+                pl.BlockSpec((near, pp*LANES), col(1)),
+                pl.BlockSpec((BLOCK, LANES), lambda h, i, f: (i, 0)),
+                pl.BlockSpec((total, LANES), lambda h, i, f: (0, 0)),
+                rowblk, rowblk,
+                pl.BlockSpec((pp, 1, 2*BLOCK, 1), lambda h, i, f: (h, i, 0, 0)),
+            ],
+            out_specs=[rowblk, both, both],
+            scratch_shapes=[
+                pltpu.VMEM((total, pp*LANES), BF),
+                pltpu.VMEM((total, pp*LANES), BF),
+                pltpu.VMEM((total, pp*LANES), F32),
+                pltpu.VMEM((total, pp*LANES), F32),
+                pltpu.VMEM((pp, BLOCK, LANES), F32),
+            ]),
+        out_shape=[
+            jax.ShapeDtypeStruct((near, width), BF),
+            jax.ShapeDtypeStruct((2, near, width), F32),
+            jax.ShapeDtypeStruct((2, near, width), BF),
+        ],
+        compiler_params=pltpu.CompilerParams(vmem_limit_bytes=56<<20),
+        cost_estimate=pl.CostEstimate(flops=10*near*total*width, bytes_accessed=16*near*width*2, transcendentals=near*total*width//64),
+        name="attn_backward",
+    )(flags, q, kv, kv, far, far, feat, hot, attn, dattn, lse)
 
 
 class Links:
@@ -239,48 +453,34 @@
 
     query_seg = row_segs(net.c)
     key_seg = jnp.concatenate([query_seg, row_segs(1 - net.c)])
-    label_row = jnp.arange(labels, dtype=F32)
-
-    def parent_of(seg):
-        return jnp.sum(
-            jnp.where(seg[:, None] == label_row[None, :], parent_row[None, :], 0.0), axis=1
-        )
-
-    first_up = parent_of(query_seg)
-    second_up = parent_of(first_up)
-    allowed = (
-        (key_seg[None, :] == query_seg[:, None])
-        | (key_seg[None, :] == first_up[:, None])
-        | (key_seg[None, :] == second_up[:, None])
-    )
+    lanes = jnp.arange(LANES, dtype=F32)
+    table = jnp.zeros((LANES,), F32).at[:labels].set(parent_row)
+    up_two = jnp.sum(jnp.where(table[:, None] == lanes[None, :], table[None, :], 0.0), axis=1)
+    reach = (
+        (lanes[:, None] == lanes[None, :])
+        | (table[:, None] == lanes[None, :])
+        | (up_two[:, None] == lanes[None, :])
+    )
+    hot = (key_seg[:, None] == lanes[None, :]).astype(BF)
+    feat = mm(hot[:mine], jnp.where(reach, 0.0, BIG).astype(BF)).astype(BF)
+    held = jnp.max(hot.reshape(-1, BLOCK, LANES), axis=1)
+    wanted = mm(held[: mine // BLOCK], reach.astype(BF)).astype(BF)
+    active = mm_t(wanted, held) > 0.5
 
     tok_f = tok.astype(F32)
     normed_one, inv_one = layer_norm(tok_f)
     lifted_one = normed_one * gain_a
     act_one = (lifted_one * (1.0 + scale_one) + shift_one).astype(BF)
-    qkv = mm(act_one, qkv_w).astype(BF)
-    kv = qkv[:, width:]
-    whole_kv = jnp.concatenate([kv, net.swap(kv)], axis=0)
-
-    def heads_of(x):
-        return x.reshape(x.shape[0], HEADS, head_dim).transpose(1, 0, 2)
-
-    query_heads = heads_of(qkv[:, :width])
-    key_heads = heads_of(whole_kv[:, :width])
-    val_heads = heads_of(whole_kv[:, width:])
-
-    def head_forward(unused, items):
-        q_h, k_h, v_h = items
-        masked = jnp.where(allowed, mm_t(q_h, k_h) * scale, -1000000000.0)
-        top_val = jnp.max(masked, axis=-1, keepdims=True)
-        expo = jnp.exp(masked - top_val)
-        row_total = jnp.sum(expo, axis=-1, keepdims=True)
-        probs = expo / row_total
-        head_out = mm(probs.astype(BF), v_h)
-        return unused, (head_out.astype(BF), top_val + jnp.log(row_total))
-
-    _, (attn_heads, log_totals) = lax.scan(head_forward, 0, (query_heads, key_heads, val_heads))
-    attn = attn_heads.transpose(1, 0, 2).reshape(mine, width)
+    kv = mm(act_one, qkv_w[:, width:]).astype(BF)
+    far = net.swap(kv)
+    query = mm(act_one, qkv_w[:, :width]).astype(BF)
+    bound = jnp.maximum(jnp.max(jnp.abs(query)), jnp.max(jnp.abs(kv))).astype(F32)
+    other_bound = jnp.maximum(bound, jnp.max(jnp.abs(far)).astype(F32))
+    safe = bound * other_bound * (head_dim * scale) < 2.0**27
+    flags = jnp.concatenate(
+        [(active | ~safe).reshape(-1), safe[None]]
+    ).astype(jnp.int32)
+    attn, log_totals = attn_fwd(query, kv, far, feat, hot, flags, scale, PAIRS)
     branch_one = mm(attn, out_w)
     middle = tok_f + gate_one * branch_one
     normed_two, inv_two = layer_norm(middle)
@@ -309,30 +509,12 @@
     grad_y1 = (grad_mid * gate_one).astype(BF)
     d_gate_one = jnp.sum(grad_mid * branch_one, axis=0)
     t_out = net.reduce_grad(t_mm(attn, grad_y1).astype(BF))
-    grad_attn = heads_of(mm_t(grad_y1, out_w).astype(BF))
-
-    def head_backward(unused, items):
-        q_h, k_h, v_h, lse_h, da_h = items
-        masked = jnp.where(allowed, mm_t(q_h, k_h) * scale, -1000000000.0)
-        again = jnp.exp(masked - lse_h)
-        grad_prob = mm_t(da_h, v_h)
-        delta_row = jnp.sum(again * grad_prob, axis=-1, keepdims=True)
-        grad_score = (again * (grad_prob - delta_row)).astype(BF)
-        grad_q = mm(grad_score, k_h) * scale
-        grad_k = t_mm(grad_score, q_h) * scale
-        grad_v = t_mm(again.astype(BF), da_h)
-        return unused, (grad_q.astype(BF), grad_k, grad_v)
-
-    _, (q_grads, k_grads, v_grads) = lax.scan(
-        head_backward, 0, (query_heads, key_heads, val_heads, log_totals, grad_attn)
-    )
-
-    def rows_of(x):
-        return x.transpose(1, 0, 2).reshape(x.shape[1], width)
-
-    tree_kv = jnp.concatenate([rows_of(k_grads), rows_of(v_grads)], axis=1)
-    local_kv = tree_kv[:mine] + net.swap(tree_kv[mine:].astype(BF)).astype(F32)
-    grad_qkv = jnp.concatenate([rows_of(q_grads), local_kv.astype(BF)], axis=1)
+    grad_attn = mm_t(grad_y1, out_w).astype(BF)
+    q_grads, near_grads, far_grads = attn_bwd(
+        query, kv, far, feat, hot, flags, attn, grad_attn, log_totals, scale, PAIRS
+    )
+    kv_grads = (near_grads + net.swap(far_grads).astype(F32)).astype(BF)
+    grad_qkv = jnp.concatenate([q_grads, kv_grads[0], kv_grads[1]], axis=1)
     t_qkv = net.reduce_grad(t_mm(act_one, grad_qkv).astype(BF))
     grad_a1 = mm_t(grad_qkv, qkv_w)
     d_shift_one = jnp.sum(grad_a1, axis=0)

time: 1020 us -> 713 us (0.70)
  matrix products: 450 us -> 103 us
  Pallas kernels: 0 us -> 131 us
  other arithmetic: 159 us -> 46.6 us
  waiting for transfers between devices: 133 us -> 237 us
  local copies, waits for them, and re-layouts: 116 us -> 44 us
    dot_general x40 -> x5, matrix products: 207 us -> 33.5 us  [mm_t(): lax.dot_general(left, right, (((1,), (1,)), ((), ())), preferred_element_...]
    pallas_call x0 -> x2, Pallas kernels: none -> 131 us  [the longest x1 86.7 us: attn_bwd(): pl.pallas_call(functools.partial(bwd_kernel, near, pp, scale), grid_spec=...]
    dot_general x28 -> x4, matrix products: 131 us -> 20.9 us  [t_mm(): lax.dot_general(left, right, (((0,), (0,)), ((), ())), preferred_element_...]
    convert_element_type x13 -> x3, other arithmetic: 105 us -> 2.43 us  [the longest x1 1.14 us: on_device(): hot = (key_seg[:, None] == lanes[None, :]).astype(BF)]
    all_gather x4, waiting for transfers between devices: 14.1 us -> 116 us  [gather_weight(): return lax.all_gather(part, ('shard', 'group'), axis=0, tiled=True)]
    dot_general x28 -> x6, matrix products: 109 us -> 44.7 us  [mm(): return jnp.dot(left, right, preferred_element_type=F32)]
    unnamed x157 -> x152, local copies, waits for them, and re-layouts: 41.2 us -> 5.99 us
    reduce_sum x14 -> x1, other arithmetic: 16 us -> 0.17 us  [on_device(): jnp.sum(jnp.where(table[:, None] == lanes[None, :], table[None, :], 0.0),...]
  transfers between devices with their start and end apart: 84 -> 84, of which waited for: 28 -> 27; matrix products, arithmetic and copies ran while one was open for 66% -> 20% of each run, Pallas kernels for 0% -> 19%
where the time goes in v2:
time: 713 us; the launch traced here: 706 us
  waiting for transfers between devices  237 us (33%)
  Pallas kernels  131 us (18%)
  starting transfers between devices  127 us (18%)
  matrix products  103 us (14%)
  other arithmetic  46.6 us (7%)
  local copies, waits for them, and re-layouts  44 us (6%)
  between operations  18.3 us (3%)
    all_gather x4, waiting for transfers between devices, gather_weight(): return lax.all_gather(part, ('shard', 'group'), axis=0, tiled=True)  116 us
    pallas_call x1, Pallas kernels, attn_bwd(): pl.pallas_call(functools.partial(bwd_kernel, near, pp, scale), grid_spec=...  86.7 us
    ppermute x27, waiting for transfers between devices, across(): lax.ppermute(value, 'group', [(i, i ^ 2 * step) for i in range(self.group...  61.8 us
    dot_general x6, matrix products, mm(): return jnp.dot(left, right, preferred_element_type=F32)  44.7 us
    pallas_call x1, Pallas kernels, attn_fwd(): pl.pallas_call(functools.partial(fwd_kernel, near, pp, scale), grid_spec=...  44.2 us
    ppermute x24, starting transfers between devices, turn(): return lax.ppermute(value, 'shard', [(i, (i + step) % n) for i in range(n)])  41.5 us
    dot_general x5, matrix products, mm_t(): lax.dot_general(left, right, (((1,), (1,)), ((), ())), preferred_element_...  33.5 us
    ppermute x8, waiting for transfers between devices, to_trees(): got.append(lax.ppermute(piece, ('group', 'shard'), self.round_perm(k)))  27.7 us
  transfers between devices with their start and end apart: 84, of which 27 were waited for; matrix products, arithmetic and copies ran while one was open for 20% of the time, Pallas kernels for 19%

profile of v2, /device:TPU:1, one launch (start us, length us, event | category | flops | bytes accessed | tf_op | source)
XLA Modules:
  0.0 706.1 jit_solution(9866080164561577171)
XLA Ops:
  15.0 4.6 collective-permute-start
  21.0 2.8 collective-permute-start.5
  23.8 2.2 collective-permute-start.7
  27.6 4.8 collective-permute-done.5
  32.5 5.6 collective-permute-start.2
  41.5 6.4 collective-permute-done.2
  47.9 21.3 %collective-permute-done.3 = bf16[256,768]{1,0:T(8,128)(2,1)S(1)} collective-permute-done((bf16[256,768]{1,0:T(8,128)(2,1)S(1)}, bf16[256,768]{1,0:T(8,128)(2,1)S(1)}, u32[]{:S(2)}, u32[]{:S(2)}) %collective-permute-start.3) | collective-permute-done | bytes 393248 | tf_op jit(solution)/shard_map/ppermute | solution.py:298
  70.1 19.3 %all-gather.5.cloned.1.call-done = bf16[768,2304]{1,0:T(8,128)(2,1)} async-done(((bf16[24,2304]{1,0:T(8,128)(2,1)}), bf16[768,2304]{1,0:T(8,128)(2,1)}) %all-gather.5.cloned.1.call-update) | async-done | bytes 3538960 | tf_op jit(solution)/shard_map/all_gather | solution.py:326
  89.5 8.2 %abs_reduce_fusion.1 = (bf16[]{:T(256)}, bf16[1024,1536]{1,0:T(8,128)(2,1)}) fusion(bf16[768,2304]{1,0:T(8,128)(2,1)} %all-gather.5.cloned.1.call-done, f32[768]{0:T(1024)S(1)} %get-tuple-element.198, f32[768]{0:T(1024)S(1)} %get-tuple-element.199, f32[768]{0:T(1024)S(1)} %mul.245, f32[1024]{0:T(1024)S(1)} %add_rsqrt_fusion.1, ...), kind=kOutput, calls=%fused_computation.59 | convolution fusion | flops 2431647744 | bytes 7095298 | tf_op jit(solution)/shard_map/dot_general | solution.py:48
  99.1 2.7 collective-permute-start.13
  101.8 2.4 collective-permute-start.14
  104.2 3.0 collective-permute-start.15
  114.9 6.2 abs_reduce_fusion.2
  122.5 2.9 abs_reduce_fusion
  127.1 44.2 %attn_forward.1 = (bf16[1024,768]{1,0:T(8,128)(2,1)}, f32[6,4,512,1]{3,2,1,0:T(8,128)}) custom-call(s32[33]{0:T(128)} %add_convert_fusion.3.flags, bf16[1024,768]{1,0:T(8,128)(2,1)} %get-tuple-element.212.q_ref, bf16[1024,1536]{1,0:T(8,128)(2,1)} %get-tuple-element.214.kn_ref.vn_ref, bf16[1024,1536]{1,0:T(8,128)(2,1)} %get-tuple-element.214.kn_ref.vn_ref, ...), custom_call_target="tpu_custom_call" | custom-call | flops 6442450944 | bytes 12582912 | tf_op jit(solution)/shard_map/attn_forward/pallas_call | solution.py:130
  171.3 5.2 fusion.103
  177.0 45.3 %all-gather.9.cloned.1.call-done = bf16[768,3072]{1,0:T(8,128)(2,1)} async-done(((bf16[24,3072]{1,0:T(8,128)(2,1)}), bf16[768,3072]{1,0:T(8,128)(2,1)}) %all-gather.9.cloned.1.call-update) | async-done | bytes 4718608 | tf_op jit(solution)/shard_map/all_gather | solution.py:326
  222.3 13.6 %multiply_convert_fusion = (bf16[1024,3072]{1,0:T(8,128)(2,1)}, f32[1024,3072]{1,0:T(8,128)}) fusion(f32[3072]{0:T(1024)} %add.606, bf16[768,3072]{1,0:T(8,128)(2,1)} %all-gather.9.cloned.1.call-done, f32[1024,768]{1,0:T(8,128)S(1)} %get-tuple-element.105, f32[768]{0:T(1024)} %get-tuple-element.196, f32[768]{0:T(1024)S(1)} %get-tuple-element.197, ...), kind=kOutput, calls=%fused_computation.10 | convolution fusion | flops 4868014080 | bytes 26768384 | tf_op jit(solution)/shard_map/dot_general | solution.py:48
  236.0 51.6 %all-gather.11.cloned.1.call-done = bf16[3072,768]{1,0:T(8,128)(2,1)} async-done(((bf16[96,768]{1,0:T(8,128)(2,1)}), bf16[3072,768]{1,0:T(8,128)(2,1)}) %all-gather.11.cloned.1.call-update) | async-done | bytes 4718608 | tf_op jit(solution)/shard_map/all_gather | solution.py:326
  287.6 18.4 %convert_reduce_fusion = (f32[3072]{0:T(1024)S(1)}, bf16[1024,3072]{1,0:T(8,128)(2,1)}) fusion(f32[1024,3072]{1,0:T(8,128)} %get-tuple-element.217, f32[3072]{0:T(1024)} %add.606, bf16[3072,768]{1,0:T(8,128)(2,1)} %all-gather.11.cloned.1.call-done, f32[768]{0:T(1024)} %get-tuple-element.195, bf16[256,768]{1,0:T(8,128)(2,1)} %collective-permute-done.16, ...), kind=kOutput, calls=%fused_computation.9 | convolution fusion | flops 4908905472 | bytes 25193472 | tf_op jit(solution)/shard_map/dot_general | solution.py:52
  306.0 7.5 %fusion.108 = f32[1024,768]{1,0:T(8,128)S(1)} fusion(bf16[1024,3072]{1,0:T(8,128)(2,1)} %get-tuple-element.220, bf16[768,3072]{1,0:T(8,128)(2,1)S(1)} %copy-done.53), kind=kOutput, calls=%fused_computation.319 | convolution fusion | flops 4831838208 | bytes 14155776 | tf_op jit(solution)/shard_map/dot_general | solution.py:52
  313.5 10.4 %convert_reduce_fusion.2 = (f32[768]{0:T(1024)S(1)}, f32[768]{0:T(1024)S(1)}, bf16[1024,768]{1,0:T(8,128)(2,1)S(1)}, f32[768]{0:T(1024)S(1)}, f32[1024]{0:T(1024...) fusion(f32[768]{0:T(1024)S(1)} %copy-done.46, bf16[256,768]{1,0:T(8,128)(2,1)} %collective-permute-done.16, ...), kind=kOutput, calls=%fused_computation.49 | convolution fusion | flops 4856210432 | bytes 20491264 | tf_op jit(solution)/shard_map/dot_general | solution.py:48
  324.0 4.1 multiply_reduce_fusion.2
  330.4 2.1 collective-permute-start.28
  332.5 6.1 convolution_convert_fusion.1
  338.7 8.1 %convolution_convert_fusion = bf16[3072,768]{1,0:T(8,128)(2,1)S(1)} fusion(bf16[1024,3072]{1,0:T(8,128)(2,1)S(1)} %bitcast.280, f32[768]{0:T(1024)S(1)} %copy-done.46, bf16[256,768]{1,0:T(8,128)(2,1)} %collective-permute-done.16, bf16[256,768]{1,0:T(8,128)(2,1)} %collective-permute-done.15, bf16[256,768]{1,0:T(8,128)(2,1)} %collective-permute-done.14, ...), kind=kOutput, calls=%fused_computation.12 | convolution fusion | flops 4842061824 | bytes 12585984 | tf_op jit(solution)/shard_map/dot_general | solution.py:56
  354.3 2.6 convolution_convert_fusion.4.do_ref
  360.7 2.6 collective-permute-start.29
  366.2 86.7 %attn_backward.1 = (bf16[1024,768]{1,0:T(8,128)(2,1)}, f32[2,1024,768]{2,1,0:T(8,128)}, bf16[2,1024,768]{2,1,0:T(8,128)(2,1)}) custom-call(s32[33]{0:T(128)} %add_convert_fusion.3.flags, bf16[1024,768]{1,0:T(8,128)(2,1)} %get-tuple-element.212.q_ref, bf16[1024,1536]{1,0:T(8,128)(2,1)} %get-tuple-element.214.kn_ref.vn_ref, ...), custom_call_target="tpu_custom_call" | custom-call | flops 16106127360 | bytes 25165824 | tf_op jit(solution)/shard_map/attn_backward/pallas_call | solution.py:231
  455.0 3.8 collective-permute-done.46
  464.4 2.8 collective-permute-done.10
  468.6 9.3 %collective-permute-done.48 = bf16[24,768]{1,0:T(8,128)(2,1)S(1)} collective-permute-done((bf16[24,768]{1,0:T(8,128)(2,1)S(1)}, bf16[24,768]{1,0:T(8,128)(2,1)S(1)}, u32[]{:S(2)}, u32[]{:S(2)}) %collective-permute-start.48) | collective-permute-done | bytes 36896 | tf_op jit(solution)/shard_map/ppermute | solution.py:278
  477.9 5.8 collective-permute-start.50
  485.4 2.1 collective-permute-start.52
  488.8 5.9 collective-permute-start.17
  494.7 3.8 collective-permute-start.12
  498.8 2.3 fusion.7
  502.6 2.6 fusion.8
  508.9 6.9 collective-permute-done.70
  519.9 9.1 %collective-permute-done.72 = bf16[4,96,768]{2,1,0:T(8,128)(2,1)S(1)} collective-permute-done((bf16[4,96,768]{2,1,0:T(8,128)(2,1)S(1)}, bf16[4,96,768]{2,1,0:T(8,128)(2,1)S(1)}, u32[]{:S(2)}, u32[]{:S(2)}) %collective-permute-start.72) | collective-permute-done | bytes 589856 | tf_op jit(solution)/shard_map/ppermute | solution.py:281
  529.3 3.4 collective-permute-start.73
  532.7 8.4 %collective-permute-done.56 = bf16[4,24,3072]{2,1,0:T(8,128)(2,1)S(1)} collective-permute-done((bf16[4,24,3072]{2,1,0:T(8,128)(2,1)S(1)}, bf16[4,24,3072]{2,1,0:T(8,128)(2,1)S(1)}, u32[]{:S(2)}, u32[]{:S(2)}) %collective-permute-start.56) | collective-permute-done | bytes 589856 | tf_op jit(solution)/shard_map/ppermute | solution.py:281
  541.1 2.3 collective-permute-start.74
  543.3 11.9 %collective-permute-done.57 = bf16[4,24,3072]{2,1,0:T(8,128)(2,1)S(1)} collective-permute-done((bf16[4,24,3072]{2,1,0:T(8,128)(2,1)S(1)}, bf16[4,24,3072]{2,1,0:T(8,128)(2,1)S(1)}, u32[]{:S(2)}, u32[]{:S(2)}) %collective-permute-start.57) | collective-permute-done | bytes 589856 | tf_op jit(solution)/shard_map/ppermute | solution.py:281
  561.2 3.3 collective-permute-done.59
  565.0 4.6 collective-permute-done.60
  573.6 4.7 fusion.20
  578.3 3.7 collective-permute-start.22
  582.1 3.1 collective-permute-start.23
  585.5 5.2 convolution_convert_fusion.2
  590.7 3.0 fusion.25
  604.0 2.1 collective-permute-start.32
  613.9 2.5 collective-permute-start.33
  616.9 4.1 collective-permute-start.18
  622.0 3.3 collective-permute-start.66
  629.6 3.5 collective-permute-start.19
  633.1 4.7 collective-permute-start.20
  647.3 2.4 fusion.70
  658.5 5.2 collective-permute-done.34
  664.7 9.2 %collective-permute-done.36 = bf16[4,24,2304]{2,1,0:T(8,128)(2,1)S(1)} collective-permute-done((bf16[4,24,2304]{2,1,0:T(8,128)(2,1)S(1)}, bf16[4,24,2304]{2,1,0:T(8,128)(2,1)S(1)}, u32[]{:S(2)}, u32[]{:S(2)}) %collective-permute-start.36) | collective-permute-done | bytes 442400 | tf_op jit(solution)/shard_map/ppermute | solution.py:281
  675.2 2.3 collective-permute-start.39
  680.1 2.5 collective-permute-start.65
  690.1 1.9 collective-permute-done.42
  692.2 2.3 collective-permute-start.43
  (440 shorter events, 132.8 us)
Async XLA Ops:
  7.3 82.2 %all-gather.5.cloned.1.call-start = ((), (), s32[]{:S(2)}) async-start(), calls=%async_computation | async-start | bytes 3649536 | tf_op jit(solution)/shard_map/all_gather | solution.py:326
  9.0 162.3 %all-gather.7.cloned.1.call-start = ((), (), s32[]{:S(2)}) async-start(), calls=%async_computation.1 | async-start | bytes 1216512 | tf_op jit(solution)/shard_map/all_gather | solution.py:326
  10.4 211.9 %all-gather.9.cloned.1.call-start = ((), (), s32[]{:S(2)}) async-start(), calls=%async_computation.2 | async-start | bytes 4866048 | tf_op jit(solution)/shard_map/all_gather | solution.py:326
  11.2 276.4 %all-gather.11.cloned.1.call-start = ((), (), s32[]{:S(2)}) async-start(), calls=%async_computation.3 | async-start | bytes 4866048 | tf_op jit(solution)/shard_map/all_gather | solution.py:326
  15.0 26.4 %collective-permute-start = (bf16[256,768]{1,0:T(8,128)(2,1)S(1)}, bf16[256,768]{1,0:T(8,128)(2,1)S(1)}, u32[]{:S(2)}, u32[]{:S(2)}) collective-permute-start(bf16[256,768]{1,0:T(8,128)(2,1)S(1)} %get-tuple-element.135), channel_id=1, source_target_pairs={{0,0},{1,4},{2,2},{3,6},{4,1},{5,5},{6,3},{7,7},{8,8},{9,12},{10,1... | collective-permute-start | bytes 1179656 | tf_op jit(solution)/shard_map/ppermute | solution.py:298
  19.6 21.8 %collective-permute-start.1 = (bf16[256,768]{1,0:T(8,128)(2,1)S(1)}, bf16[256,768]{1,0:T(8,128)(2,1)S(1)}, u32[]{:S(2)}, u32[]{:S(2)}) collective-permute-start(bf16[256,768]{1,0:T(8,128)(2,1)S(1)} %get-tuple-element.138), channel_id=1, source_target_pairs={{0,4},{1,2},{2,6},{3,0},{4,5},{5,3},{6,7},{7,1},{8,12},{9,10},{10,... | collective-permute-start | bytes 1179656 | tf_op jit(solution)/shard_map/ppermute | solution.py:298
  21.0 11.4 %collective-permute-start.5 = (f32[2496]{0:T(1024)S(1)}, f32[2496]{0:T(1024)S(1)}, u32[]{:S(2)}, u32[]{:S(2)}) collective-permute-start(f32[2496]{0:T(1024)S(1)} %get-tuple-element.99), channel_id=1, source_target_pairs={{0,1},{1,2},{2,3},{3,0},{4,5},{5,6},{6,7},{7,4},{8,9},{9,10},{10,1... | collective-permute-start | bytes 29960 | tf_op jit(solution)/shard_map/ppermute | solution.py:278
  23.8 14.3 %collective-permute-start.6 = (f32[2496]{0:T(1024)S(1)}, f32[2496]{0:T(1024)S(1)}, u32[]{:S(2)}, u32[]{:S(2)}) collective-permute-start(f32[2496]{0:T(1024)S(1)} %get-tuple-element.101), channel_id=1, source_target_pairs={{0,2},{1,3},{2,0},{3,1},{4,6},{5,7},{6,4},{7,5},{8,10},{9,11},{10,... | collective-permute-start | bytes 29960 | tf_op jit(solution)/shard_map/ppermute | solution.py:278
  23.8 16.1 %collective-permute-start.7 = (f32[2496]{0:T(1024)S(1)}, f32[2496]{0:T(1024)S(1)}, u32[]{:S(2)}, u32[]{:S(2)}) collective-permute-start(f32[2496]{0:T(1024)S(1)} %get-tuple-element.100), channel_id=1, source_target_pairs={{0,3},{1,0},{2,1},{3,2},{4,7},{5,4},{6,5},{7,6},{8,11},{9,8},{10,9... | collective-permute-start | bytes 29960 | tf_op jit(solution)/shard_map/ppermute | solution.py:278
  32.5 15.4 %collective-permute-start.2 = (bf16[256,768]{1,0:T(8,128)(2,1)S(1)}, bf16[256,768]{1,0:T(8,128)(2,1)S(1)}, u32[]{:S(2)}, u32[]{:S(2)}) collective-permute-start(bf16[256,768]{1,0:T(8,128)(2,1)S(1)} %get-tuple-element.137), channel_id=1, source_target_pairs={{0,2},{1,6},{2,0},{3,4},{4,3},{5,7},{6,1},{7,5},{8,10},{9,14},{10,... | collective-permute-start | bytes 1179656 | tf_op jit(solution)/shard_map/ppermute | solution.py:298
  38.1 31.1 %collective-permute-start.3 = (bf16[256,768]{1,0:T(8,128)(2,1)S(1)}, bf16[256,768]{1,0:T(8,128)(2,1)S(1)}, u32[]{:S(2)}, u32[]{:S(2)}) collective-permute-start(bf16[256,768]{1,0:T(8,128)(2,1)S(1)} %get-tuple-element.136), channel_id=1, source_target_pairs={{0,6},{1,0},{2,4},{3,2},{4,7},{5,1},{6,5},{7,3},{8,14},{9,8},{10,1... | collective-permute-start | bytes 1179656 | tf_op jit(solution)/shard_map/ppermute | solution.py:298
  97.6 24.8 %collective-permute-start.8 = (bf16[1024,1536]{1,0:T(8,128)(2,1)}, bf16[1024,1536]{1,0:T(8,128)(2,1)}, u32[]{:S(2)}, u32[]{:S(2)}) collective-permute-start(bf16[1024,1536]{1,0:T(8,128)(2,1)} %get-tuple-element.214.kn_ref.vn_ref), channel_id=1, source_target_pairs={{0,4},{4,0},{8,12},{12,8},{16,20},{20,16},{24,28},{28,24},{1,5},{5... | collective-permute-start | bytes 9437192 | tf_op jit(solution)/shard_map/ppermute | solution.py:274
  99.1 136.9 %collective-permute-start.13 = (bf16[256,768]{1,0:T(8,128)(2,1)}, bf16[256,768]{1,0:T(8,128)(2,1)}, u32[]{:S(2)}, u32[]{:S(2)}) collective-permute-start(bf16[256,768]{1,0:T(8,128)(2,1)} %get-tuple-element.127), channel_id=1, source_target_pairs={{0,0},{1,4},{2,2},{3,6},{4,1},{5,5},{6,3},{7,7},{8,8},{9,12},{10,1... | collective-permute-start | bytes 1179656 | tf_op jit(solution)/shard_map/ppermute | solution.py:298
  101.8 134.2 %collective-permute-start.14 = (bf16[256,768]{1,0:T(8,128)(2,1)}, bf16[256,768]{1,0:T(8,128)(2,1)}, u32[]{:S(2)}, u32[]{:S(2)}) collective-permute-start(bf16[256,768]{1,0:T(8,128)(2,1)} %get-tuple-element.130), channel_id=1, source_target_pairs={{0,4},{1,2},{2,6},{3,0},{4,5},{5,3},{6,7},{7,1},{8,12},{9,10},{10,... | collective-permute-start | bytes 1179656 | tf_op jit(solution)/shard_map/ppermute | solution.py:298
  104.2 131.8 %collective-permute-start.15 = (bf16[256,768]{1,0:T(8,128)(2,1)}, bf16[256,768]{1,0:T(8,128)(2,1)}, u32[]{:S(2)}, u32[]{:S(2)}) collective-permute-start(bf16[256,768]{1,0:T(8,128)(2,1)} %get-tuple-element.129), channel_id=1, source_target_pairs={{0,2},{1,6},{2,0},{3,4},{4,3},{5,7},{6,1},{7,5},{8,10},{9,14},{10,... | collective-permute-start | bytes 1179656 | tf_op jit(solution)/shard_map/ppermute | solution.py:298
  107.2 128.7 %collective-permute-start.16 = (bf16[256,768]{1,0:T(8,128)(2,1)}, bf16[256,768]{1,0:T(8,128)(2,1)}, u32[]{:S(2)}, u32[]{:S(2)}) collective-permute-start(bf16[256,768]{1,0:T(8,128)(2,1)} %get-tuple-element.128), channel_id=1, source_target_pairs={{0,6},{1,0},{2,4},{3,2},{4,7},{5,1},{6,5},{7,3},{8,14},{9,8},{10,1... | collective-permute-start | bytes 1179656 | tf_op jit(solution)/shard_map/ppermute | solution.py:298
  328.3 28.8 %collective-permute-start.26 = (f32[7680]{0:T(1024)S(1)}, f32[7680]{0:T(1024)S(1)}, u32[]{:S(2)}, u32[]{:S(2)}) collective-permute-start(f32[7680]{0:T(1024)S(1)} %constant_dynamic-update-slice_fusion.11), channel_id=1, source_target_pairs={{0,1},{1,2},{2,3},{3,0},{4,5},{5,6},{6,7},{7,4},{8,9},{9,10},{10,1... | collective-permute-start | bytes 92168 | tf_op jit(solution)/shard_map/ppermute | solution.py:278
  329.9 27.7 %collective-permute-start.27 = (f32[7680]{0:T(1024)S(1)}, f32[7680]{0:T(1024)S(1)}, u32[]{:S(2)}, u32[]{:S(2)}) collective-permute-start(f32[7680]{0:T(1024)S(1)} %constant_dynamic-update-slice_fusion.11), channel_id=1, source_target_pairs={{0,2},{1,3},{2,0},{3,1},{4,6},{5,7},{6,4},{7,5},{8,10},{9,11},{10,... | collective-permute-start | bytes 92168 | tf_op jit(solution)/shard_map/ppermute | solution.py:278
  330.4 29.2 %collective-permute-start.28 = (f32[7680]{0:T(1024)S(1)}, f32[7680]{0:T(1024)S(1)}, u32[]{:S(2)}, u32[]{:S(2)}) collective-permute-start(f32[7680]{0:T(1024)S(1)} %constant_dynamic-update-slice_fusion.11), channel_id=1, source_target_pairs={{0,3},{1,0},{2,1},{3,2},{4,7},{5,4},{6,5},{7,6},{8,11},{9,8},{10,9... | collective-permute-start | bytes 92168 | tf_op jit(solution)/shard_map/ppermute | solution.py:278
  348.4 150.4 %collective-permute-start.69 = (bf16[4,384,768]{2,1,0:T(8,128)(2,1)}, bf16[4,384,768]{2,1,0:T(8,128)(2,1)}, u32[]{:S(2)}, u32[]{:S(2)}) collective-permute-start(bf16[4,384,768]{2,1,0:T(8,128)(2,1)} %dynamic-slice_bitcast_fusion), channel_id=1, source_target_pairs={{0,4},{4,0},{8,12},{12,8},{16,20},{20,16},{24,28},{28,24},{1,5},{5... | collective-permute-start | bytes 7077896 | tf_op jit(solution)/shard_map/ppermute | solution.py:274
  351.0 151.6 %collective-permute-start.55 = (bf16[4,96,3072]{2,1,0:T(8,128)(2,1)}, bf16[4,96,3072]{2,1,0:T(8,128)(2,1)}, u32[]{:S(2)}, u32[]{:S(2)}) collective-permute-start(bf16[4,96,3072]{2,1,0:T(8,128)(2,1)} %dynamic-slice_bitcast_fusion.1), channel_id=1, source_target_pairs={{0,4},{4,0},{8,12},{12,8},{16,20},{20,16},{24,28},{28,24},{1,5},{5... | collective-permute-start | bytes 7077896 | tf_op jit(solution)/shard_map/ppermute | solution.py:274
  357.7 102.7 %collective-permute-start.9 = (bf16[256,768]{1,0:T(8,128)(2,1)}, bf16[256,768]{1,0:T(8,128)(2,1)}, u32[]{:S(2)}, u32[]{:S(2)}) collective-permute-start(bf16[256,768]{1,0:T(8,128)(2,1)} %get-tuple-element.134), channel_id=1, source_target_pairs={{0,0},{4,1},{2,2},{6,3},{1,4},{5,5},{3,6},{7,7},{8,8},{12,9},{10,1... | collective-permute-start | bytes 1179656 | tf_op jit(solution)/shard_map/ppermute | solution.py:307
  360.7 92.2 %collective-permute-start.29 = (f32[4,7680]{1,0:T(4,128)}, f32[4,7680]{1,0:T(4,128)}, u32[]{:S(2)}, u32[]{:S(2)}) collective-permute-start(f32[4,7680]{1,0:T(4,128)} %pad_maximum_fusion.18), channel_id=1, source_target_pairs={{0,4},{4,0},{8,12},{12,8},{16,20},{20,16},{24,28},{28,24},{1,5},{5... | collective-permute-start | bytes 368648 | tf_op jit(solution)/shard_map/ppermute | solution.py:274
  365.1 88.0 %collective-permute-start.45 = (bf16[4,24,768]{2,1,0:T(8,128)(2,1)}, bf16[4,24,768]{2,1,0:T(8,128)(2,1)}, u32[]{:S(2)}, u32[]{:S(2)}) collective-permute-start(bf16[4,24,768]{2,1,0:T(8,128)(2,1)} %get-tuple-element.157), channel_id=1, source_target_pairs={{0,8},{4,12},{8,0},{12,4},{16,24},{20,28},{24,16},{28,20},{1,9},{5... | collective-permute-start | bytes 442376 | tf_op jit(solution)/shard_map/ppermute | solution.py:281
  458.8 8.4 %collective-permute-start.10 = (bf16[256,768]{1,0:T(8,128)(2,1)}, bf16[256,768]{1,0:T(8,128)(2,1)S(1)}, u32[]{:S(2)}, u32[]{:S(2)}) collective-permute-start(bf16[256,768]{1,0:T(8,128)(2,1)} %get-tuple-element.133), channel_id=1, source_target_pairs={{4,0},{2,1},{6,2},{0,3},{5,4},{3,5},{7,6},{1,7},{12,8},{10,9},{14,... | collective-permute-start | bytes 1179656 | tf_op jit(solution)/shard_map/ppermute | solution.py:307
  458.8 28.7 %collective-permute-start.11 = (bf16[256,768]{1,0:T(8,128)(2,1)}, bf16[256,768]{1,0:T(8,128)(2,1)S(1)}, u32[]{:S(2)}, u32[]{:S(2)}) collective-permute-start(bf16[256,768]{1,0:T(8,128)(2,1)} %get-tuple-element.132), channel_id=1, source_target_pairs={{2,0},{6,1},{0,2},{4,3},{3,4},{7,5},{1,6},{5,7},{10,8},{14,9},{8,1... | collective-permute-start | bytes 1179656 | tf_op jit(solution)/shard_map/ppermute | solution.py:307
  460.3 17.6 %collective-permute-start.48 = (bf16[24,768]{1,0:T(8,128)(2,1)S(1)}, bf16[24,768]{1,0:T(8,128)(2,1)S(1)}, u32[]{:S(2)}, u32[]{:S(2)}) collective-permute-start(bf16[24,768]{1,0:T(8,128)(2,1)S(1)} %get-tuple-element.171), channel_id=1, source_target_pairs={{0,1},{1,2},{2,3},{3,0},{4,5},{5,6},{6,7},{7,4},{8,9},{9,10},{10,1... | collective-permute-start | bytes 110600 | tf_op jit(solution)/shard_map/ppermute | solution.py:278
  467.2 17.2 %collective-permute-start.49 = (bf16[24,768]{1,0:T(8,128)(2,1)S(1)}, bf16[24,768]{1,0:T(8,128)(2,1)S(1)}, u32[]{:S(2)}, u32[]{:S(2)}) collective-permute-start(bf16[24,768]{1,0:T(8,128)(2,1)S(1)} %get-tuple-element.173), channel_id=1, source_target_pairs={{0,2},{1,3},{2,0},{3,1},{4,6},{5,7},{6,4},{7,5},{8,10},{9,11},{10,... | collective-permute-start | bytes 110600 | tf_op jit(solution)/shard_map/ppermute | solution.py:278
  485.4 9.3 %collective-permute-start.52 = (bf16[24,768]{1,0:T(8,128)(2,1)S(1)}, bf16[24,768]{1,0:T(8,128)(2,1)S(1)}, u32[]{:S(2)}, u32[]{:S(2)}) collective-permute-start(bf16[24,768]{1,0:T(8,128)(2,1)S(1)} %fusion.69), channel_id=1, source_target_pairs={{0,16},{4,20},{8,24},{12,28},{16,0},{20,4},{24,8},{28,12},{1,17},{... | collective-permute-start | bytes 110600 | tf_op jit(solution)/shard_map/ppermute | solution.py:281
  487.6 11.0 %collective-permute-start.53 = (bf16[24,768]{1,0:T(8,128)(2,1)S(1)}, bf16[24,768]{1,0:T(8,128)(2,1)S(1)}, u32[]{:S(2)}, u32[]{:S(2)}) collective-permute-start(bf16[24,768]{1,0:T(8,128)(2,1)S(1)} %fusion.69), channel_id=1, source_target_pairs={{0,24},{4,28},{8,16},{12,20},{16,8},{20,12},{24,0},{28,4},{1,25},{... | collective-permute-start | bytes 110600 | tf_op jit(solution)/shard_map/ppermute | solution.py:281
  488.8 81.6 %collective-permute-start.17 = (bf16[2,1024,768]{2,1,0:T(8,128)(2,1)S(1)}, bf16[2,1024,768]{2,1,0:T(8,128)(2,1)S(1)}, u32[]{:S(2)}, u32[]{:S(2)}) collective-permute-start(bf16[2,1024,768]{2,1,0:T(8,128)(2,1)S(1)} %copy-done.56), channel_id=1, source_target_pairs={{0,4},{4,0},{8,12},{12,8},{16,20},{20,16},{24,28},{28,24},{1,5},{5... | collective-permute-start | bytes 9437192 | tf_op jit(solution)/shard_map/ppermute | solution.py:274
  494.7 11.9 %collective-permute-start.12 = (bf16[256,768]{1,0:T(8,128)(2,1)S(1)}, bf16[256,768]{1,0:T(8,128)(2,1)S(1)}, u32[]{:S(2)}, u32[]{:S(2)}) collective-permute-start(bf16[256,768]{1,0:T(8,128)(2,1)S(1)} %copy-done.24), channel_id=1, source_target_pairs={{6,0},{0,1},{4,2},{2,3},{7,4},{1,5},{5,6},{3,7},{14,8},{8,9},{12,1... | collective-permute-start | bytes 1179656 | tf_op jit(solution)/shard_map/ppermute | solution.py:307
  498.7 8.9 %collective-permute-start.54 = (bf16[96,768]{1,0:T(8,128)(2,1)S(1)}, bf16[96,768]{1,0:T(8,128)(2,1)S(1)}, u32[]{:S(2)}, u32[]{:S(2)}) collective-permute-start(bf16[96,768]{1,0:T(8,128)(2,1)S(1)} %bitcast.245), channel_id=1, source_target_pairs={{0,4},{4,0},{8,12},{12,8},{16,20},{20,16},{24,28},{28,24},{1,5},{5... | collective-permute-start | bytes 442376 | tf_op jit(solution)/shard_map/ppermute | solution.py:274
  501.2 14.5 %collective-permute-start.70 = (bf16[4,96,768]{2,1,0:T(8,128)(2,1)S(1)}, bf16[4,96,768]{2,1,0:T(8,128)(2,1)S(1)}, u32[]{:S(2)}, u32[]{:S(2)}) collective-permute-start(bf16[4,96,768]{2,1,0:T(8,128)(2,1)S(1)} %get-tuple-element.114), channel_id=1, source_target_pairs={{0,8},{4,12},{8,0},{12,4},{16,24},{20,28},{24,16},{28,20},{1,9},{5... | collective-permute-start | bytes 1769480 | tf_op jit(solution)/shard_map/ppermute | solution.py:281
  502.6 14.6 %collective-permute-start.71 = (bf16[4,96,768]{2,1,0:T(8,128)(2,1)S(1)}, bf16[4,96,768]{2,1,0:T(8,128)(2,1)S(1)}, u32[]{:S(2)}, u32[]{:S(2)}) collective-permute-start(bf16[4,96,768]{2,1,0:T(8,128)(2,1)S(1)} %get-tuple-element.116), channel_id=1, source_target_pairs={{0,16},{4,20},{8,24},{12,28},{16,0},{20,4},{24,8},{28,12},{1,17},{... | collective-permute-start | bytes 1769480 | tf_op jit(solution)/shard_map/ppermute | solution.py:281
  506.6 22.3 %collective-permute-start.72 = (bf16[4,96,768]{2,1,0:T(8,128)(2,1)S(1)}, bf16[4,96,768]{2,1,0:T(8,128)(2,1)S(1)}, u32[]{:S(2)}, u32[]{:S(2)}) collective-permute-start(bf16[4,96,768]{2,1,0:T(8,128)(2,1)S(1)} %get-tuple-element.115), channel_id=1, source_target_pairs={{0,24},{4,28},{8,16},{12,20},{16,8},{20,12},{24,0},{28,4},{1,25},{... | collective-permute-start | bytes 1769480 | tf_op jit(solution)/shard_map/ppermute | solution.py:281
  507.6 33.5 %collective-permute-start.56 = (bf16[4,24,3072]{2,1,0:T(8,128)(2,1)S(1)}, bf16[4,24,3072]{2,1,0:T(8,128)(2,1)S(1)}, u32[]{:S(2)}, u32[]{:S(2)}) collective-permute-start(bf16[4,24,3072]{2,1,0:T(8,128)(2,1)S(1)} %get-tuple-element.117), channel_id=1, source_target_pairs={{0,8},{4,12},{8,0},{12,4},{16,24},{20,28},{24,16},{28,20},{1,9},{5... | collective-permute-start | bytes 1769480 | tf_op jit(solution)/shard_map/ppermute | solution.py:281
  515.7 39.5 %collective-permute-start.57 = (bf16[4,24,3072]{2,1,0:T(8,128)(2,1)S(1)}, bf16[4,24,3072]{2,1,0:T(8,128)(2,1)S(1)}, u32[]{:S(2)}, u32[]{:S(2)}) collective-permute-start(bf16[4,24,3072]{2,1,0:T(8,128)(2,1)S(1)} %get-tuple-element.119), channel_id=1, source_target_pairs={{0,16},{4,20},{8,24},{12,28},{16,0},{20,4},{24,8},{28,12},{1,17},{... | collective-permute-start | bytes 1769480 | tf_op jit(solution)/shard_map/ppermute | solution.py:281
  517.2 38.7 %collective-permute-start.58 = (bf16[4,24,3072]{2,1,0:T(8,128)(2,1)S(1)}, bf16[4,24,3072]{2,1,0:T(8,128)(2,1)S(1)}, u32[]{:S(2)}, u32[]{:S(2)}) collective-permute-start(bf16[4,24,3072]{2,1,0:T(8,128)(2,1)S(1)} %get-tuple-element.118), channel_id=1, source_target_pairs={{0,24},{4,28},{8,16},{12,20},{16,8},{20,12},{24,0},{28,4},{1,25},{... | collective-permute-start | bytes 1769480 | tf_op jit(solution)/shard_map/ppermute | solution.py:281
  529.3 27.9 %collective-permute-start.73 = (bf16[96,768]{1,0:T(8,128)(2,1)S(1)}, bf16[96,768]{1,0:T(8,128)(2,1)S(1)}, u32[]{:S(2)}, u32[]{:S(2)}) collective-permute-start(bf16[96,768]{1,0:T(8,128)(2,1)S(1)} %get-tuple-element.147), channel_id=1, source_target_pairs={{0,1},{1,2},{2,3},{3,0},{4,5},{5,6},{6,7},{7,4},{8,9},{9,10},{10,1... | collective-permute-start | bytes 442376 | tf_op jit(solution)/shard_map/ppermute | solution.py:278
  541.1 17.6 %collective-permute-start.74 = (bf16[96,768]{1,0:T(8,128)(2,1)S(1)}, bf16[96,768]{1,0:T(8,128)(2,1)S(1)}, u32[]{:S(2)}, u32[]{:S(2)}) collective-permute-start(bf16[96,768]{1,0:T(8,128)(2,1)S(1)} %get-tuple-element.149), channel_id=1, source_target_pairs={{0,2},{1,3},{2,0},{3,1},{4,6},{5,7},{6,4},{7,5},{8,10},{9,11},{10,... | collective-permute-start | bytes 442376 | tf_op jit(solution)/shard_map/ppermute | solution.py:278
  556.3 8.2 %collective-permute-start.59 = (bf16[24,3072]{1,0:T(8,128)(2,1)S(1)}, bf16[24,3072]{1,0:T(8,128)(2,1)S(1)}, u32[]{:S(2)}, u32[]{:S(2)}) collective-permute-start(bf16[24,3072]{1,0:T(8,128)(2,1)S(1)} %get-tuple-element.154), channel_id=1, source_target_pairs={{0,1},{1,2},{2,3},{3,0},{4,5},{5,6},{6,7},{7,4},{8,9},{9,10},{10,1... | collective-permute-start | bytes 442376 | tf_op jit(solution)/shard_map/ppermute | solution.py:278
  557.2 12.4 %collective-permute-start.60 = (bf16[24,3072]{1,0:T(8,128)(2,1)S(1)}, bf16[24,3072]{1,0:T(8,128)(2,1)S(1)}, u32[]{:S(2)}, u32[]{:S(2)}) collective-permute-start(bf16[24,3072]{1,0:T(8,128)(2,1)S(1)} %get-tuple-element.156), channel_id=1, source_target_pairs={{0,2},{1,3},{2,0},{3,1},{4,6},{5,7},{6,4},{7,5},{8,10},{9,11},{10,... | collective-permute-start | bytes 442376 | tf_op jit(solution)/shard_map/ppermute | solution.py:278
  558.7 10.9 %collective-permute-start.61 = (bf16[24,3072]{1,0:T(8,128)(2,1)S(1)}, bf16[24,3072]{1,0:T(8,128)(2,1)S(1)}, u32[]{:S(2)}, u32[]{:S(2)}) collective-permute-start(bf16[24,3072]{1,0:T(8,128)(2,1)S(1)} %get-tuple-element.155), channel_id=1, source_target_pairs={{0,3},{1,0},{2,1},{3,2},{4,7},{5,4},{6,5},{7,6},{8,11},{9,8},{10,9... | collective-permute-start | bytes 442376 | tf_op jit(solution)/shard_map/ppermute | solution.py:278
  560.4 61.6 %collective-permute-start.76 = (bf16[96,768]{1,0:T(8,128)(2,1)}, bf16[96,768]{1,0:T(8,128)(2,1)}, u32[]{:S(2)}, u32[]{:S(2)}) collective-permute-start(bf16[96,768]{1,0:T(8,128)(2,1)} %fusion.57), channel_id=1, source_target_pairs={{0,8},{4,12},{8,0},{12,4},{16,24},{20,28},{24,16},{28,20},{1,9},{5... | collective-permute-start | bytes 442376 | tf_op jit(solution)/shard_map/ppermute | solution.py:281
  564.6 60.8 %collective-permute-start.77 = (bf16[96,768]{1,0:T(8,128)(2,1)}, bf16[96,768]{1,0:T(8,128)(2,1)}, u32[]{:S(2)}, u32[]{:S(2)}) collective-permute-start(bf16[96,768]{1,0:T(8,128)(2,1)} %fusion.57), channel_id=1, source_target_pairs={{0,16},{4,20},{8,24},{12,28},{16,0},{20,4},{24,8},{28,12},{1,17},{... | collective-permute-start | bytes 442376 | tf_op jit(solution)/shard_map/ppermute | solution.py:281
  578.3 16.7 %collective-permute-start.22 = (f32[2304]{0:T(1024)S(1)}, f32[2304]{0:T(1024)S(1)}, u32[]{:S(2)}, u32[]{:S(2)}) collective-permute-start(f32[2304]{0:T(1024)S(1)} %pad_maximum_fusion.25), channel_id=1, source_target_pairs={{0,1},{1,2},{2,3},{3,0},{4,5},{5,6},{6,7},{7,4},{8,9},{9,10},{10,1... | collective-permute-start | bytes 27656 | tf_op jit(solution)/shard_map/ppermute | solution.py:278
  582.1 13.0 %collective-permute-start.23 = (f32[2304]{0:T(1024)S(1)}, f32[2304]{0:T(1024)S(1)}, u32[]{:S(2)}, u32[]{:S(2)}) collective-permute-start(f32[2304]{0:T(1024)S(1)} %pad_maximum_fusion.25), channel_id=1, source_target_pairs={{0,2},{1,3},{2,0},{3,1},{4,6},{5,7},{6,4},{7,5},{8,10},{9,11},{10,... | collective-permute-start | bytes 27656 | tf_op jit(solution)/shard_map/ppermute | solution.py:278
  585.2 9.9 %collective-permute-start.24 = (f32[2304]{0:T(1024)S(1)}, f32[2304]{0:T(1024)S(1)}, u32[]{:S(2)}, u32[]{:S(2)}) collective-permute-start(f32[2304]{0:T(1024)S(1)} %pad_maximum_fusion.25), channel_id=1, source_target_pairs={{0,3},{1,0},{2,1},{3,2},{4,7},{5,4},{6,5},{7,6},{8,11},{9,8},{10,9... | collective-permute-start | bytes 27656 | tf_op jit(solution)/shard_map/ppermute | solution.py:278
  613.0 13.3 %collective-permute-start.78 = (bf16[96,768]{1,0:T(8,128)(2,1)}, bf16[96,768]{1,0:T(8,128)(2,1)S(1)}, u32[]{:S(2)}, u32[]{:S(2)}) collective-permute-start(bf16[96,768]{1,0:T(8,128)(2,1)} %fusion.57), channel_id=1, source_target_pairs={{0,24},{4,28},{8,16},{12,20},{16,8},{20,12},{24,0},{28,4},{1,25},{... | collective-permute-start | bytes 442376 | tf_op jit(solution)/shard_map/ppermute | solution.py:281
  613.9 35.7 %collective-permute-start.33 = (bf16[4,96,2304]{2,1,0:T(8,128)(2,1)}, bf16[4,96,2304]{2,1,0:T(8,128)(2,1)}, u32[]{:S(2)}, u32[]{:S(2)}) collective-permute-start(bf16[4,96,2304]{2,1,0:T(8,128)(2,1)} %dynamic-slice_bitcast_fusion.2), channel_id=1, source_target_pairs={{0,4},{4,0},{8,12},{12,8},{16,20},{20,16},{24,28},{28,24},{1,5},{5... | collective-permute-start | bytes 5308424 | tf_op jit(solution)/shard_map/ppermute | solution.py:274
  616.9 36.0 %collective-permute-start.18 = (bf16[256,768]{1,0:T(8,128)(2,1)}, bf16[256,768]{1,0:T(8,128)(2,1)}, u32[]{:S(2)}, u32[]{:S(2)}) collective-permute-start(bf16[256,768]{1,0:T(8,128)(2,1)} %get-tuple-element.126), channel_id=1, source_target_pairs={{0,0},{4,1},{2,2},{6,3},{1,4},{5,5},{3,6},{7,7},{8,8},{12,9},{10,1... | collective-permute-start | bytes 1179656 | tf_op jit(solution)/shard_map/ppermute | solution.py:307
  625.3 7.8 %collective-permute-start.67 = (f32[4,10112]{1,0:T(4,128)S(1)}, f32[4,10112]{1,0:T(4,128)S(1)}, u32[]{:S(2)}, u32[]{:S(2)}) collective-permute-start(f32[4,10112]{1,0:T(4,128)S(1)} %get-tuple-element.179), channel_id=1, source_target_pairs={{0,16},{4,20},{8,24},{12,28},{16,0},{20,4},{24,8},{28,12},{1,17},{... | collective-permute-start | bytes 485384 | tf_op jit(solution)/shard_map/ppermute | solution.py:281
  626.3 11.5 %collective-permute-start.68 = (f32[4,10112]{1,0:T(4,128)S(1)}, f32[4,10112]{1,0:T(4,128)S(1)}, u32[]{:S(2)}, u32[]{:S(2)}) collective-permute-start(f32[4,10112]{1,0:T(4,128)S(1)} %get-tuple-element.179), channel_id=1, source_target_pairs={{0,24},{4,28},{8,16},{12,20},{16,8},{20,12},{24,0},{28,4},{1,25},{... | collective-permute-start | bytes 485384 | tf_op jit(solution)/shard_map/ppermute | solution.py:281
  629.6 26.0 %collective-permute-start.19 = (bf16[256,768]{1,0:T(8,128)(2,1)}, bf16[256,768]{1,0:T(8,128)(2,1)}, u32[]{:S(2)}, u32[]{:S(2)}) collective-permute-start(bf16[256,768]{1,0:T(8,128)(2,1)} %get-tuple-element.125), channel_id=1, source_target_pairs={{4,0},{2,1},{6,2},{0,3},{5,4},{3,5},{7,6},{1,7},{12,8},{10,9},{14,... | collective-permute-start | bytes 1179656 | tf_op jit(solution)/shard_map/ppermute | solution.py:307
  633.1 42.1 %collective-permute-start.20 = (bf16[256,768]{1,0:T(8,128)(2,1)}, bf16[256,768]{1,0:T(8,128)(2,1)}, u32[]{:S(2)}, u32[]{:S(2)}) collective-permute-start(bf16[256,768]{1,0:T(8,128)(2,1)} %get-tuple-element.124), channel_id=1, source_target_pairs={{2,0},{6,1},{0,2},{4,3},{3,4},{7,5},{1,6},{5,7},{10,8},{14,9},{8,1... | collective-permute-start | bytes 1179656 | tf_op jit(solution)/shard_map/ppermute | solution.py:307
  651.7 12.0 %collective-permute-start.34 = (bf16[4,24,2304]{2,1,0:T(8,128)(2,1)S(1)}, bf16[4,24,2304]{2,1,0:T(8,128)(2,1)S(1)}, u32[]{:S(2)}, u32[]{:S(2)}) collective-permute-start(bf16[4,24,2304]{2,1,0:T(8,128)(2,1)S(1)} %get-tuple-element.120), channel_id=1, source_target_pairs={{0,8},{4,12},{8,0},{12,4},{16,24},{20,28},{24,16},{28,20},{1,9},{5... | collective-permute-start | bytes 1327112 | tf_op jit(solution)/shard_map/ppermute | solution.py:281
  651.8 12.9 %collective-permute-start.35 = (bf16[4,24,2304]{2,1,0:T(8,128)(2,1)S(1)}, bf16[4,24,2304]{2,1,0:T(8,128)(2,1)S(1)}, u32[]{:S(2)}, u32[]{:S(2)}) collective-permute-start(bf16[4,24,2304]{2,1,0:T(8,128)(2,1)S(1)} %get-tuple-element.122), channel_id=1, source_target_pairs={{0,16},{4,20},{8,24},{12,28},{16,0},{20,4},{24,8},{28,12},{1,17},{... | collective-permute-start | bytes 1327112 | tf_op jit(solution)/shard_map/ppermute | solution.py:281
  652.8 21.1 %collective-permute-start.36 = (bf16[4,24,2304]{2,1,0:T(8,128)(2,1)S(1)}, bf16[4,24,2304]{2,1,0:T(8,128)(2,1)S(1)}, u32[]{:S(2)}, u32[]{:S(2)}) collective-permute-start(bf16[4,24,2304]{2,1,0:T(8,128)(2,1)S(1)} %get-tuple-element.121), channel_id=1, source_target_pairs={{0,24},{4,28},{8,16},{12,20},{16,8},{20,12},{24,0},{28,4},{1,25},{... | collective-permute-start | bytes 1327112 | tf_op jit(solution)/shard_map/ppermute | solution.py:281
  655.6 31.9 %collective-permute-start.21 = (bf16[256,768]{1,0:T(8,128)(2,1)S(1)}, bf16[256,768]{1,0:T(8,128)(2,1)S(1)}, u32[]{:S(2)}, u32[]{:S(2)}) collective-permute-start(bf16[256,768]{1,0:T(8,128)(2,1)S(1)} %copy-done.23), channel_id=1, source_target_pairs={{6,0},{0,1},{4,2},{2,3},{7,4},{1,5},{5,6},{3,7},{14,8},{8,9},{12,1... | collective-permute-start | bytes 1179656 | tf_op jit(solution)/shard_map/ppermute | solution.py:307
  663.7 30.8 %collective-permute-start.79 = (bf16[384,768]{1,0:T(8,128)(2,1)S(1)}, bf16[384,768]{1,0:T(8,128)(2,1)S(1)}, u32[]{:S(2)}, u32[]{:S(2)}) collective-permute-start(bf16[384,768]{1,0:T(8,128)(2,1)S(1)} %bitcast.235), channel_id=1, source_target_pairs={{0,4},{4,0},{8,12},{12,8},{16,20},{20,16},{24,28},{28,24},{1,5},{5... | collective-permute-start | bytes 1769480 | tf_op jit(solution)/shard_map/ppermute | solution.py:274
  674.5 10.0 %collective-permute-start.38 = (bf16[24,2304]{1,0:T(8,128)(2,1)S(1)}, bf16[24,2304]{1,0:T(8,128)(2,1)S(1)}, u32[]{:S(2)}, u32[]{:S(2)}) collective-permute-start(bf16[24,2304]{1,0:T(8,128)(2,1)S(1)} %get-tuple-element.166), channel_id=1, source_target_pairs={{0,2},{1,3},{2,0},{3,1},{4,6},{5,7},{6,4},{7,5},{8,10},{9,11},{10,... | collective-permute-start | bytes 331784 | tf_op jit(solution)/shard_map/ppermute | solution.py:278
  675.2 9.4 %collective-permute-start.39 = (bf16[24,2304]{1,0:T(8,128)(2,1)S(1)}, bf16[24,2304]{1,0:T(8,128)(2,1)S(1)}, u32[]{:S(2)}, u32[]{:S(2)}) collective-permute-start(bf16[24,2304]{1,0:T(8,128)(2,1)S(1)} %get-tuple-element.165), channel_id=1, source_target_pairs={{0,3},{1,0},{2,1},{3,2},{4,7},{5,4},{6,5},{7,6},{8,11},{9,8},{10,9... | collective-permute-start | bytes 331784 | tf_op jit(solution)/shard_map/ppermute | solution.py:278
  680.1 16.0 %collective-permute-start.65 = (bf16[96,3072]{1,0:T(8,128)(2,1)S(1)}, bf16[96,3072]{1,0:T(8,128)(2,1)S(1)}, u32[]{:S(2)}, u32[]{:S(2)}) collective-permute-start(bf16[96,3072]{1,0:T(8,128)(2,1)S(1)} %bitcast.233), channel_id=1, source_target_pairs={{0,4},{4,0},{8,12},{12,8},{16,20},{20,16},{24,28},{28,24},{1,5},{5... | collective-permute-start | bytes 1769480 | tf_op jit(solution)/shard_map/ppermute | solution.py:274
  (89 other events, 1918.3 us)
Sparse Core Ops, SparseCore 0:
  11.6 77.8 all-gather.4
  92.4 64.4 all-gather.6
  159.8 62.5 all-gather.8
  225.1 62.4 all-gather.10
